TPU v7x, 128 devices: a whole 4x4x4 slice. The times are simulated.
128 devices in a mesh: tm: 16 (over x_hi, y, core), input: 8 (over x_lo, z).
Axes of the slice: x: 4 (x_hi: 2, x_lo: 2; x = x_hi * 2 + x_lo), y: 4, z: 4, core: 2. Of those that a mesh axis runs over, the one named last changes fastest.
Arguments:
- samples: int32 [1024, 262144], P('input', 'tm'), may hold values from -16 to 16, as said below
- coefficients: float32 [8, 512], replicated, may hold values from -2 to 2
Outputs:
- visibility: bfloat16 [256, 2, 1024, 1024], P(('tm', 'input'))
Inputs may be any that keep to these rules, and one draw needn't show every extreme that they name: `samples`: noise-dominated integer voltages: each input carries independent integer noise plus a weak common signal.
All inputs are finite; a program needn't handle non-finite values.
Results may differ from a plain program's by a relative error of at most 0.007.
Values may be sent and summed in bfloat16 or wider, within the bound.
No kernel may reach another device: no remote copies, remote signals or barrier semaphores. Data moves between devices by JAX's collectives and lax.ppermute only.
A program may use at most 128 MiB of HBM per device.

v0:
```python
import math

import jax
import jax.numpy as jnp
from jax import lax
from jax.sharding import PartitionSpec as P


def from_behind(block, axis, distance):
    devices = range(lax.axis_size(axis))
    route = [(i - distance, i) for i in devices if i - distance in devices]
    return lax.ppermute(block, axis, route)


def dft_table(length):
    row_index = jnp.arange(length, dtype=jnp.int32)
    channel = row_index // 2
    parity = row_index % 2
    positions = jnp.arange(length, dtype=jnp.int32)
    phase_index = channel[:, None] * positions[None, :] % length
    angles = phase_index.astype(jnp.float32) * (2.0 * math.pi / length)
    values = jnp.where(parity[:, None] == 0, jnp.cos(angles), -jnp.sin(angles)) / math.sqrt(length)
    return values.astype(jnp.bfloat16)


def local(samples, coefficients):
    inputs_dev, sample_count = samples.shape
    tap_count, fft_length = coefficients.shape
    frames_dev = sample_count // fft_length
    tm_count = lax.axis_size("tm")
    input_count = lax.axis_size("input")
    devices = tm_count * input_count
    frames_all = frames_dev * tm_count
    signal = (samples.astype(jnp.float32) / 8.0).reshape(inputs_dev, frames_dev, fft_length)
    tail_frames = signal[:, frames_dev - (tap_count - 1) :, :].astype(jnp.bfloat16)
    previous = from_behind(tail_frames, "tm", 1)
    extended = jnp.concatenate([previous.astype(jnp.float32), signal], axis=1)
    filtered = jnp.zeros((inputs_dev, frames_dev, fft_length), jnp.float32)
    for tap_index in range(tap_count):
        start_frame = tap_count - 1 - tap_index
        filtered = (
            filtered
            + coefficients[tap_index][None, None, :]
            * extended[:, start_frame : start_frame + frames_dev, :]
        )
    filtered = filtered.astype(jnp.bfloat16)
    spectra = jnp.einsum(
        "mn,ifn->mfi", dft_table(fft_length), filtered, preferred_element_type=jnp.float32
    ).astype(jnp.bfloat16)
    channels = fft_length // 2
    per_device = channels // devices
    outgoing = spectra.reshape(1, devices, per_device, 2 * frames_dev, inputs_dev)
    received = lax.all_to_all(outgoing, ("tm", "input"), split_axis=1, concat_axis=0, tiled=True)
    item_count = received.shape[-3]
    spectra_block = received.reshape(tm_count, input_count, item_count, 2, frames_dev, inputs_dev)
    real_part = jnp.einsum(
        "tacrfi,tbcrfj->caibj", spectra_block, spectra_block, preferred_element_type=jnp.float32
    )
    cross_part = jnp.einsum(
        "tacfi,tbcfj->caibj",
        spectra_block[:, :, :, 1],
        spectra_block[:, :, :, 0],
        preferred_element_type=jnp.float32,
    )
    imag_part = cross_part - jnp.transpose(cross_part, (0, 3, 4, 1, 2))
    full_width = input_count * inputs_dev
    stacked = jnp.stack([real_part, imag_part], axis=1).reshape(
        item_count, 2, full_width, full_width
    )
    return (stacked / frames_all).astype(jnp.bfloat16)


def solution(mesh):
    in_specs = (P("input", "tm"), P())
    out_specs = P(("tm", "input"), None, None, None)
    return jax.shard_map(local, mesh=mesh, in_specs=in_specs, out_specs=out_specs, check_vma=False)
```

profile of v0, /device:TPU:0, one launch (start us, length us, event | category | flops | bytes accessed | tf_op | source)
XLA Modules:
  0.0 219.6 jit_solution(17197157155315856110)
XLA Ops:
  0.0 4.1 %convert_multiply_fusion = f32[128,16384]{1,0:T(8,128)S(1)} fusion(s32[128,16384]{1,0:T(8,128)} %param.2), kind=kLoop, calls=%fused_computation.38 | loop fusion | flops 4194304 | bytes 16777216 | tf_op jit(solution)/shard_map/div | solution.py:34
  4.1 0.0 copy-start.2
  4.1 1.4 copy.54
  5.5 0.0 copy-start.1
  5.6 3.4 %copy-done.1 = f32[16,32,8,512]{3,2,0,1:T(8,128)} copy-done((f32[16,32,8,512]{3,2,0,1:T(8,128)}, f32[16,32,8,512]{3,2,0,1:T(8,128)S(1)}, u32[]{:S(2)}) %copy-start.1) | copy-done | bytes 8388632
  8.9 0.1 slice.199
  9.1 1.3 collective-permute-start
  10.4 0.0 copy-done.2
  10.5 2.0 collective-permute-done
  12.4 0.2 convert_element_type.26
  12.7 26.9 %convert_bitcast_fusion = bf16[512,32,128]{0,2,1:T(8,128)(2,1)} fusion(f32[128,32,512]{2,0,1:T(8,128)} %bitcast.51, f32[128,7,512]{2,0,1:T(8,128)S(1)} %convert_element_type.26, f32[512]{0:T(512)S(1)} %bitcast.58, f32[512]{0:T(512)S(1)} %bitcast.59, f32[512]{0:T(512)S(1)} %bitcast.53, f32[512]{0:T(512)S(1)} %bitcast.54, f32[512]{0:T(512)S(1)} %bitcast.55, ...), kind=kOutput, calls=%fused_computation.42 | convolution fusion | flops 2202533888 | bytes 14436864 | tf_op jit(solution)/shard_map/mn,ifn->mfi/dot_general | solution.py:47
  39.6 7.8 %copy.22 = bf16[512,32,128]{2,1,0:T(8,128)(2,1)} copy(bf16[512,32,128]{0,2,1:T(8,128)(2,1)} %convert_bitcast_fusion) | data formatting | bytes 8388608 | tf_op jit(solution)/shard_map/convert_element_type | solution.py:49
  47.4 75.7 %all_to_all.4 = bf16[1,128,2,64,128]{4,3,2,0,1:T(8,128)(2,1)S(1)} all-to-all(bf16[1,128,2,64,128]{4,3,2,0,1:T(8,128)(2,1)} %bitcast.49), channel_id=1, replica_groups=mesh['tm'=16,'input'=8] {'tm','input'}, dimensions={1} | all-to-all | bytes 8388608 | tf_op jit(solution)/shard_map/all_to_all | solution.py:53
  123.1 0.0 copy-start
  123.2 2.0 copy-done
  125.1 1.4 fusion.61
  126.5 5.8 %convolution_bitcast_fusion = f32[2,8,128,8,128]{4,2,3,1,0:T(8,128)} fusion(bf16[16,8,2,1,32,128]{5,4,3,2,1,0:T(8,128)(2,1)S(1)} %get-tuple-element.6, bf16[16,8,2,1,32,128]{5,4,3,2,1,0:T(8,128)(2,1)S(1)} %get-tuple-element.5), kind=kOutput, calls=%fused_computation.45 | convolution fusion | flops 2147483648 | bytes 12582912 | tf_op jit(solution)/shard_map/tacfi,tbcfj->caibj/dot_general | solution.py:59
  132.3 8.7 %copy.27 = f32[2,8,128,8,128]{2,4,1,3,0:T(8,128)} copy(f32[2,8,128,8,128]{4,2,3,1,0:T(8,128)} %convolution_bitcast_fusion) | data formatting | bytes 16777216 | tf_op jit(solution)/shard_map/tacfi,tbcfj->caibj/dot_general | solution.py:59
  141.0 11.9 %bitcast_subtract_fusion = f32[2,8,128,8,128]{4,2,3,1,0:T(8,128)} fusion(f32[2,8,128,8,128]{4,2,3,1,0:T(8,128)} %convolution_bitcast_fusion, f32[2,8,128,8,128]{2,4,1,3,0:T(8,128)} %copy.27), kind=kLoop, calls=%fused_computation.37 | loop fusion | flops 2097152 | bytes 25165824 | tf_op jit(solution)/shard_map/sub | solution.py:65
  152.9 13.2 %copy.28 = f32[2,8,128,8,128]{4,3,2,1,0:T(8,128)} copy(f32[2,8,128,8,128]{4,2,3,1,0:T(8,128)} %bitcast_subtract_fusion) | data formatting | bytes 16777216 | tf_op jit(solution)/shard_map/sub | solution.py:65
  166.0 9.2 %stack.10 = f32[2,1,1024,1024]{3,2,0,1:T(8,128)} reshape(f32[2,8,128,8,128]{4,3,2,1,0:T(8,128)} %copy.28) | data formatting | bytes 16777216 | tf_op jit(solution)/shard_map/stack | solution.py:67
  175.3 7.8 %fusion.27 = f32[2,8,128,8,128]{4,2,3,1,0:T(8,128)S(1)} fusion(bf16[16,8,2,2,32,128,1]{5,4,3,2,1,0,6:T(8,128)(2,1)} %bitcast.48), kind=kOutput, calls=%fused_computation.44 | convolution fusion | flops 4294967296 | bytes 12582912 | tf_op jit(solution)/shard_map/tacrfi,tbcrfj->caibj/dot_general | solution.py:56
  183.1 9.8 %copy.24 = f32[2,8,128,8,128]{4,3,2,1,0:T(8,128)} copy(f32[2,8,128,8,128]{4,2,3,1,0:T(8,128)S(1)} %fusion.27) | data formatting | bytes 16777216 | tf_op jit(solution)/shard_map/tacrfi,tbcrfj->caibj/dot_general | solution.py:56
  192.8 9.3 %stack.9 = f32[2,1,1024,1024]{3,2,0,1:T(8,128)} reshape(f32[2,8,128,8,128]{4,3,2,1,0:T(8,128)} %copy.24) | data formatting | bytes 16777216 | tf_op jit(solution)/shard_map/stack | solution.py:67
  202.1 9.7 %fusion = bf16[2,2,1024,1024]{3,2,0,1:T(8,128)(2,1)} fusion(f32[2,1,1024,1024]{3,2,0,1:T(8,128)} %stack.10, f32[2,1,1024,1024]{3,2,0,1:T(8,128)} %stack.9), kind=kLoop, calls=%fused_computation.7 | loop fusion | flops 12582912 | bytes 25165824 | tf_op jit(solution)/shard_map/convert_element_type | solution.py:70
  211.8 7.8 %copy.29 = bf16[2,2,1024,1024]{3,2,1,0:T(8,128)(2,1)} copy(bf16[2,2,1024,1024]{3,2,0,1:T(8,128)(2,1)} %fusion) | data formatting | bytes 16777216 | tf_op jit(solution)/shard_map/convert_element_type | solution.py:70
  (3 shorter events, 0.0 us)
Async XLA Ops:
  4.1 6.4 %copy-start.2 = (f32[8,512]{1,0:T(8,128)S(1)}, f32[8,512]{1,0:T(8,128)}, u32[]{:S(2)}) copy-start(f32[8,512]{1,0:T(8,128)} %param.3) | copy-start | bytes 49156
  5.5 3.4 %copy-start.1 = (f32[16,32,8,512]{3,2,0,1:T(8,128)}, f32[16,32,8,512]{3,2,0,1:T(8,128)S(1)}, u32[]{:S(2)}) copy-start(f32[16,32,8,512]{3,2,0,1:T(8,128)S(1)} %copy.54) | copy-start | bytes 25165828
  9.1 3.4 %collective-permute-start = (bf16[128,7,512]{2,0,1:T(8,128)(2,1)S(1)}, bf16[128,7,512]{2,0,1:T(8,128)(2,1)S(1)}, u32[]{:S(2)}, u32[]{:S(2)}) collective-permute-start(bf16[128,7,512]{2,0,1:T(8,128)(2,1)S(1)} %slice.199), channel_id=1, source_target_pairs={{0,8},{8,16},{16,24},{24,32},{32,40},{40,48},{48,56},{56,64},{64,7... | collective-permute-start | bytes 2752520 | tf_op jit(solution)/shard_map/ppermute | solution.py:12
  123.1 2.0 copy-start
where the time goes:
time: 221 us; the launch traced here: 220 us
  blocking collectives  75.7 us (34%)
  local copies, waits for them, and re-layouts  74 us (33%)
  matrix products  40.5 us (18%)
  other arithmetic  25.9 us (12%)
    all_to_all x1, blocking collectives, local(): lax.all_to_all(outgoing, ('tm', 'input'), split_axis=1, concat_axis=0, ti...  75.7 us
    dot_general x1, matrix products, local(): jnp.einsum('mn,ifn->mfi', dft_table(fft_length), filtered, preferred_elem...  26.9 us
    another operation x2, local copies, waits for them, and re-layouts, local(): jnp.stack([real_part, imag_part], axis=1)  18.5 us
    sub x1, local copies, waits for them, and re-layouts, local(): imag_part = cross_part - jnp.transpose(cross_part, (0, 3, 4, 1, 2))  13.2 us
    sub x1, other arithmetic, local(): imag_part = cross_part - jnp.transpose(cross_part, (0, 3, 4, 1, 2))  11.9 us
    dot_general x1, local copies, waits for them, and re-layouts, local(): jnp.einsum('tacrfi,tbcrfj->caibj', spectra_block, spectra_block, preferre...  9.75 us
    convert_element_type x1, other arithmetic, local(): return (stacked / frames_all).astype(jnp.bfloat16)  9.68 us
    dot_general x1, local copies, waits for them, and re-layouts, local(): jnp.einsum('tacfi,tbcfj->caibj', spectra_block[:, :, :, 1], spectra_block...  8.71 us
  transfers between devices with their start and end apart: 1, of which 1 were waited for; matrix products, arithmetic and copies ran while one was open for 0% of the time, Pallas kernels for 0%

commit v1 on v0

v1 whole, which is shorter than its diff:
```python
import functools

import jax
import jax.numpy as jnp
import ml_dtypes
import numpy as np
from jax import lax
from jax.experimental import pallas as pl
from jax.experimental.pallas import tpu as pltpu
from jax.sharding import PartitionSpec as P

GROUP = 8
BLOCK = 256


def dft_table(length):
    channel = np.arange(length) // 2
    phase = channel[:, None] * np.arange(length)[None, :] % length
    angles = phase * (2.0 * np.pi / length)
    real = (np.arange(length) % 2 == 0)[:, None]
    values = np.where(real, np.cos(angles), -np.sin(angles)) / np.sqrt(length)
    return values.astype(ml_dtypes.bfloat16)


def filter_group(cur_ref, tail, coef_ref, table_ref, out_ref, filt, spread):
    taps, fft = coef_ref.shape
    inputs = cur_ref.shape[0]
    past = taps - 1

    def rows_step(it, carry):
        rows = pl.ds(pl.multiple_of(it * 16, 16), 16)
        for n0 in range(0, fft, 128):
            coefs = [coef_ref[p : p + 1, n0 : n0 + 128] for p in range(taps)]
            window = [tail[rows, k * fft + n0 : k * fft + n0 + 128] for k in range(past)]
            for f in range(GROUP):
                window.append(cur_ref[rows, f * fft + n0 : f * fft + n0 + 128].astype(jnp.float32))
                total = coefs[0] * window[-1]
                for p in range(1, taps):
                    total = total + coefs[p] * window[-1 - p]
                filt[f, rows, n0 : n0 + 128] = total.astype(jnp.bfloat16)
                window.pop(0)
        return carry

    lax.fori_loop(0, inputs // 16, rows_step, 0)
    for f in range(0, GROUP, 2):
        pair = filt[f : f + 2].reshape(2 * inputs, fft)
        spectra = lax.dot_general(
            table_ref[...], pair, (((1,), (1,)), ((), ())), preferred_element_type=jnp.float32
        )
        spread[pl.ds(f, fft, stride=GROUP), :] = spectra[:, :inputs]
        spread[pl.ds(f + 1, fft, stride=GROUP), :] = spectra[:, inputs:]
    out_ref[...] = spread[...].reshape(fft, GROUP, inputs).astype(jnp.bfloat16)


def later_kernel(first_ref, cur_ref, coef_ref, table_ref, out_ref, tail, filt, spread):
    fft = coef_ref.shape[1]

    @pl.when(pl.program_id(0) == 0)
    def _():
        tail[...] = first_ref[:, fft:].astype(jnp.float32)

    filter_group(cur_ref, tail, coef_ref, table_ref, out_ref, filt, spread)
    tail[...] = cur_ref[:, fft:].astype(jnp.float32)


def first_kernel(halo_ref, cur_ref, coef_ref, table_ref, _, out_ref, tail, filt, spread):
    tail[...] = halo_ref[...].astype(jnp.float32)
    filter_group(cur_ref, tail, coef_ref, table_ref, out_ref, filt, spread)


def correlate_kernel(recv_ref, out_ref, held, turned, swapped):
    tm_count, input_count, _, _, frames, inputs = recv_ref.shape
    half = tm_count * frames
    width = input_count * inputs
    for r in range(2):
        for a in range(tm_count):
            for b in range(input_count):
                rows = slice(r * half + a * frames, r * half + (a + 1) * frames)
                cols = slice(b * inputs, (b + 1) * inputs)
                held[rows, cols] = recv_ref[a, b, 0, r]
    turned[...] = held[...].T
    swapped[:half] = -held[half:]
    swapped[half:] = held[:half]
    scale = 1.0 / half
    for i in range(0, width, BLOCK):
        for j in range(i, width, BLOCK):
            left = turned[i : i + BLOCK]
            real = jnp.dot(left, held[:, j : j + BLOCK], preferred_element_type=jnp.float32) * scale
            imag = jnp.dot(left, swapped[:, j : j + BLOCK], preferred_element_type=jnp.float32) * scale
            out_ref[0, 0, i : i + BLOCK, j : j + BLOCK] = real.astype(jnp.bfloat16)
            out_ref[0, 1, i : i + BLOCK, j : j + BLOCK] = imag.astype(jnp.bfloat16)
            if j > i:
                out_ref[0, 0, j : j + BLOCK, i : i + BLOCK] = real.T.astype(jnp.bfloat16)
                out_ref[0, 1, j : j + BLOCK, i : i + BLOCK] = (-imag.T).astype(jnp.bfloat16)


def local(samples, coefficients):
    inputs, sample_count = samples.shape
    taps, fft = coefficients.shape
    frames = sample_count // fft
    tm_count = lax.axis_size("tm")
    input_count = lax.axis_size("input")
    devices = tm_count * input_count
    groups = frames // GROUP
    span = GROUP * fft
    past = (taps - 1) * fft
    table = jnp.asarray(dft_table(fft))

    tail = samples[:, sample_count - past :].astype(jnp.bfloat16)
    route = [(i - 1, i) for i in range(1, tm_count)]
    halo = lax.ppermute(tail, "tm", route)
    scaled = coefficients * 0.125

    whole = lambda *shape: pl.BlockSpec(shape, lambda g: (0,) * len(shape))
    scratch = [
        pltpu.VMEM((inputs, past), jnp.float32),
        pltpu.VMEM((GROUP, inputs, fft), jnp.bfloat16),
        pltpu.VMEM((fft * GROUP, inputs), jnp.float32),
    ]
    shape = jax.ShapeDtypeStruct((fft, frames, inputs), jnp.bfloat16)
    spectra = pl.pallas_call(
        later_kernel,
        grid=(groups - 1,),
        in_specs=[
            whole(inputs, span),
            pl.BlockSpec((inputs, span), lambda g: (0, g + 1)),
            whole(taps, fft),
            whole(fft, fft),
        ],
        out_specs=pl.BlockSpec((fft, GROUP, inputs), lambda g: (0, g + 1, 0)),
        out_shape=shape,
        scratch_shapes=scratch,
        name="later_frames",
    )(samples, samples, scaled, table)
    spectra = pl.pallas_call(
        first_kernel,
        grid=(1,),
        in_specs=[
            whole(inputs, past),
            whole(inputs, span),
            whole(taps, fft),
            whole(fft, fft),
            pl.BlockSpec(memory_space=pl.ANY),
        ],
        out_specs=pl.BlockSpec((fft, GROUP, inputs), lambda g: (0, 0, 0)),
        out_shape=shape,
        scratch_shapes=scratch,
        input_output_aliases={4: 0},
        name="first_frames",
    )(halo, samples, scaled, table, spectra)

    items = fft // (2 * devices)
    outgoing = spectra.reshape(devices, 2 * items, frames, inputs)
    received = lax.all_to_all(outgoing, ("tm", "input"), 0, 0, tiled=True)
    received = received.reshape(tm_count, input_count, items, 2, frames, inputs)
    depth = 2 * tm_count * frames
    width = input_count * inputs
    return pl.pallas_call(
        correlate_kernel,
        grid=(items,),
        in_specs=[
            pl.BlockSpec(
                (tm_count, input_count, 1, 2, frames, inputs), lambda c: (0, 0, c, 0, 0, 0)
            )
        ],
        out_specs=pl.BlockSpec((1, 2, width, width), lambda c: (c, 0, 0, 0)),
        out_shape=jax.ShapeDtypeStruct((items, 2, width, width), jnp.bfloat16),
        scratch_shapes=[
            pltpu.VMEM((depth, width), jnp.bfloat16),
            pltpu.VMEM((width, depth), jnp.bfloat16),
            pltpu.VMEM((depth, width), jnp.bfloat16),
        ],
        name="correlate",
    )(received)


def solution(mesh):
    in_specs = (P("input", "tm"), P())
    out_specs = P(("tm", "input"), None, None, None)
    return jax.shard_map(local, mesh=mesh, in_specs=in_specs, out_specs=out_specs, check_vma=False)
```

time: 221 us -> 96.9 us (0.44)
  local copies, waits for them, and re-layouts: 74 us -> 0.92 us
  matrix products: 40.5 us -> 0 us
  Pallas kernels: 0 us -> 25.1 us
  other arithmetic: 25.9 us -> 2.91 us
  blocking collectives: 75.7 us -> 66.3 us
    dot_general x3 -> x0, matrix products: 40.5 us -> none  [the longest x1 26.9 us: local(): jnp.einsum('mn,ifn->mfi', dft_table(fft_length), filtered, preferred_elem...]
    pallas_call x0 -> x3, Pallas kernels: none -> 25.1 us  [the longest x1 10.2 us: local(): pl.pallas_call(later_kernel, grid=(groups - 1,), in_specs=[whole(inputs,...]
    another operation x2 -> x0, local copies, waits for them, and re-layouts: 18.5 us -> none  [local(): jnp.stack([real_part, imag_part], axis=1)]
    dot_general x2 -> x0, local copies, waits for them, and re-layouts: 18.5 us -> none  [the longest x1 9.75 us: local(): jnp.einsum('tacrfi,tbcrfj->caibj', spectra_block, spectra_block, preferre...]
    convert_element_type x2 -> x0, local copies, waits for them, and re-layouts: 15.6 us -> none  [the longest x1 7.83 us: local(): spectra = jnp.einsum('mn,ifn->mfi', dft_table(fft_length), filtered, pref...]
    sub x1 -> x0, local copies, waits for them, and re-layouts: 13.2 us -> none  [local(): imag_part = cross_part - jnp.transpose(cross_part, (0, 3, 4, 1, 2))]
    sub x1 -> x0, other arithmetic: 11.9 us -> none  [local(): imag_part = cross_part - jnp.transpose(cross_part, (0, 3, 4, 1, 2))]
    convert_element_type x2 -> x0, other arithmetic: 9.91 us -> none  [the longest x1 9.68 us: local(): return (stacked / frames_all).astype(jnp.bfloat16)]
  transfers between devices with their start and end apart: 1 -> 1, of which waited for: 1 -> 0; matrix products, arithmetic and copies ran while one was open for 0% -> 1% of each run, Pallas kernels for 0% -> 11%
where the time goes in v1:
time: 96.9 us; the launch traced here: 96.6 us
  blocking collectives  66.3 us (68%)
  Pallas kernels  25.1 us (26%)
  other arithmetic  2.91 us (3%)
  starting transfers between devices  1.35 us (1%)
    all_to_all x1, blocking collectives, local(): received = lax.all_to_all(outgoing, ('tm', 'input'), 0, 0, tiled=True)  66.3 us
    pallas_call x1, Pallas kernels, local(): pl.pallas_call(later_kernel, grid=(groups - 1,), in_specs=[whole(inputs,...  10.2 us
    pallas_call x1, Pallas kernels, local(): pl.pallas_call(correlate_kernel, grid=(items,), in_specs=[pl.BlockSpec((t...  9.7 us
    pallas_call x1, Pallas kernels, local(): pl.pallas_call(first_kernel, grid=(1,), in_specs=[whole(inputs, past), wh...  5.19 us
  transfers between devices with their start and end apart: 1, of which 0 were waited for; matrix products, arithmetic and copies ran while one was open for 1% of the time, Pallas kernels for 11%

profile of v1, /device:TPU:0, one launch (start us, length us, event | category | flops | bytes accessed | tf_op | source)
XLA Modules:
  0.0 96.6 jit_solution(1858609758286780354)
XLA Ops:
  0.0 1.6 %slice_convert_fusion = bf16[128,3584]{1,0:T(8,128)(2,1)S(1)} fusion(s32[128,16384]{1,0:T(8,128)} %cur_ref.3), kind=kLoop, calls=%fused_computation | loop fusion | flops 458752 | bytes 2752512 | tf_op jit(solution)/shard_map/convert
  1.6 1.3 %collective-permute-start = (bf16[128,3584]{1,0:T(8,128)(2,1)S(1)}, bf16[128,3584]{1,0:T(8,128)(2,1)S(1)}, u32[]{:S(2)}, u32[]{:S(2)}) collective-permute-start(bf16[128,3584]{1,0:T(8,128)(2,1)S(1)} %slice_convert_fusion), channel_id=1, source_target_pairs={{0,8},{8,16},{16,24},{24,32},{32,40},{40,48},{48,56},{56,64},{64,7... | collective-permute-start | bytes 2752520 | tf_op jit(solution)/shard_map/ppermute | solution.py:111
  3.0 1.3 %broadcast_multiply_fusion.coef_ref = f32[8,512]{1,0:T(8,128)} fusion(f32[8,512]{1,0:T(8,128)} %param.4), kind=kLoop, calls=%fused_computation.1 | loop fusion | flops 4096 | bytes 32768 | tf_op jit(solution)/shard_map/mul | solution.py:112
  4.3 10.2 %later_frames.1._ = bf16[512,32,128]{2,1,0:T(8,128)(2,1)} custom-call(s32[128,16384]{1,0:T(8,128)} %cur_ref.3, s32[128,16384]{1,0:T(8,128)} %cur_ref.3, f32[8,512]{1,0:T(8,128)} %broadcast_multiply_fusion.coef_ref, bf16[512,512]{1,0:T(8,128)(2,1)} %constant.4.clone.table_ref), custom_call_target="tpu_custom_call" | custom-call | tf_op jit(solution)/shard_map/later_frames/pallas_call | solution.py:121
  14.5 0.0 collective-permute-done.halo_ref
  14.5 0.0 copy-start
  14.5 0.9 copy-done
  15.4 5.2 %first_frames.1 = bf16[512,32,128]{2,1,0:T(8,128)(2,1)} custom-call(bf16[128,3584]{1,0:T(8,128)(2,1)} %copy-done, s32[128,16384]{1,0:T(8,128)} %cur_ref.3, f32[8,512]{1,0:T(8,128)} %broadcast_multiply_fusion.coef_ref, bf16[512,512]{1,0:T(8,128)(2,1)} %constant.4.clone.table_ref, bf16[512,32,128]{2,1,0:T(8,128)(2,1)} %later_frames.1._), custom_call_target="tpu_custom_call", output_to_operand_aliasing={{}: (4, {})} | custom-call | tf_op jit(solution)/shard_map/first_frames/pallas_call | solution.py:135
  20.6 66.3 %all_to_all.5 = bf16[128,4,32,128]{3,2,1,0:T(8,128)(2,1)} all-to-all(bf16[128,4,32,128]{3,2,1,0:T(8,128)(2,1)} %bitcast.2), channel_id=1, replica_groups=mesh['tm'=16,'input'=8] {'tm','input'}, dimensions={0} | all-to-all | bytes 8388608 | tf_op jit(solution)/shard_map/all_to_all | solution.py:154
  86.9 9.7 %correlate.1 = bf16[2,2,1024,1024]{3,2,1,0:T(8,128)(2,1)} custom-call(bf16[16,8,2,2,32,128]{5,4,3,2,1,0:T(8,128)(2,1)} %bitcast.3), custom_call_target="tpu_custom_call" | custom-call | tf_op jit(solution)/shard_map/correlate/pallas_call | solution.py:158
Async XLA Ops:
  1.6 12.9 %collective-permute-start = (bf16[128,3584]{1,0:T(8,128)(2,1)S(1)}, bf16[128,3584]{1,0:T(8,128)(2,1)S(1)}, u32[]{:S(2)}, u32[]{:S(2)}) collective-permute-start(bf16[128,3584]{1,0:T(8,128)(2,1)S(1)} %slice_convert_fusion), channel_id=1, source_target_pairs={{0,8},{8,16},{16,24},{24,32},{32,40},{40,48},{48,56},{56,64},{64,7... | collective-permute-start | bytes 2752520 | tf_op jit(solution)/shard_map/ppermute | solution.py:111
  14.5 0.9 copy-start

commit v2 on v0

v2 whole, which is shorter than its diff:
```python
import jax
import jax.numpy as jnp
import ml_dtypes
import numpy as np
from jax import lax
from jax.experimental import pallas as pl
from jax.experimental.pallas import tpu as pltpu
from jax.sharding import PartitionSpec as P

GROUP = 8
BLOCK = 256
ROWS = 16
LANES = 128


def dft_table(length):
    channel = np.arange(length) // 2
    phase = channel[:, None] * np.arange(length)[None, :] % length
    angles = phase * (2.0 * np.pi / length)
    real = (np.arange(length) % 2 == 0)[:, None]
    values = np.where(real, np.cos(angles), -np.sin(angles)) / np.sqrt(length)
    return (values.astype(ml_dtypes.bfloat16).astype(np.float32) / 8.0).astype(ml_dtypes.bfloat16)


def transform(filt, table_ref, spread, stage, spectra_ref, group, sem):
    frames, inputs, fft = filt.shape
    for f in range(0, frames, 2):
        pair = filt[f : f + 2].reshape(2 * inputs, fft)
        spectra = lax.dot_general(
            table_ref[...], pair, (((1,), (1,)), ((), ())), preferred_element_type=jnp.float32
        )
        spread[pl.ds(f, fft, stride=frames), :] = spectra[:, :inputs]
        spread[pl.ds(f + 1, fft, stride=frames), :] = spectra[:, inputs:]
    block = spread[...].reshape(fft, frames, inputs).astype(jnp.bfloat16)
    stage[...] = block
    copy = pltpu.make_async_copy(
        stage, spectra_ref.at[:, pl.ds(group * frames, frames), :], sem
    )
    copy.start()
    return copy


def own_kernel(
    samples_ref, coef_hbm, table_hbm, spectra_ref, partial_ref,
    coef_ref, table_ref, held, filt, spread, stage, sems, out_sems,
):
    taps, fft = coef_ref.shape
    groups, inputs, span = held.shape
    coef_copy = pltpu.make_async_copy(coef_hbm, coef_ref, sems.at[groups])
    coef_copy.start()
    copies = []
    for g in range(groups):
        copy = pltpu.make_async_copy(
            samples_ref.at[:, pl.ds(g * span, span)], held.at[g], sems.at[g]
        )
        copy.start()
        copies.append(copy)
    table_copy = pltpu.make_async_copy(table_hbm, table_ref, sems.at[groups + 1])
    table_copy.start()
    coef_copy.wait()
    results = []

    for g in range(groups):
        copies[g].wait()

        def rows_step(it, carry, g=g):
            rows = pl.ds(pl.multiple_of(it * ROWS, ROWS), ROWS)
            for n0 in range(0, fft, LANES):
                coefs = [coef_ref[p : p + 1, n0 : n0 + LANES] for p in range(taps)]

                def frame(f):
                    where, k = (g, f) if f >= 0 else (g - 1, f + GROUP)
                    return held[where, rows, k * fft + n0 : k * fft + n0 + LANES].astype(jnp.float32)

                window = [frame(f) for f in range(1 - taps, 0)] if g else []
                for f in range(GROUP):
                    window.append(frame(f))
                    total = coefs[0] * window[-1]
                    for p in range(1, min(taps, len(window))):
                        total = total + coefs[p] * window[-1 - p]
                    if g:
                        filt[f, rows, n0 : n0 + LANES] = total.astype(jnp.bfloat16)
                    else:
                        partial_ref[f, rows, n0 : n0 + LANES] = total
                    if len(window) == taps:
                        window.pop(0)
            return carry

        lax.fori_loop(0, inputs // ROWS, rows_step, 0)
        if g:
            if g == 1:
                table_copy.wait()
            results.append(
                transform(filt, table_ref, spread, stage.at[g - 1], spectra_ref, g, out_sems.at[g - 1])
            )
    for copy in results:
        copy.wait()


def first_kernel(
    flag_ref, halo_ref, partial_ref, coef_ref, table_ref, _, spectra_ref, filt, spread, stage, sem
):
    taps, fft = coef_ref.shape
    inputs = halo_ref.shape[0]
    past = taps - 1
    flag = flag_ref[0]

    def rows_step(it, carry):
        rows = pl.ds(pl.multiple_of(it * ROWS, ROWS), ROWS)
        for n0 in range(0, fft, LANES):
            coefs = [coef_ref[p : p + 1, n0 : n0 + LANES] * flag for p in range(taps)]
            window = [
                halo_ref[rows, k * fft + n0 : k * fft + n0 + LANES].astype(jnp.float32)
                for k in range(past)
            ]
            for f in range(GROUP):
                total = partial_ref[f, rows, n0 : n0 + LANES]
                for p in range(f + 1, taps):
                    total = total + coefs[p] * window[f - p + past]
                filt[f, rows, n0 : n0 + LANES] = total.astype(jnp.bfloat16)
        return carry

    lax.fori_loop(0, inputs // ROWS, rows_step, 0)
    transform(filt, table_ref, spread, stage, spectra_ref, 0, sem).wait()


def correlate_kernel(recv_ref, out_ref, held, turned, swapped, stage, sems):
    tm_count, input_count, items, _, frames, inputs = recv_ref.shape
    half = tm_count * frames
    width = input_count * inputs
    scale = 1.0 / half
    copies = []

    def give(c, part, i, j, value):
        rows, cols = pl.ds(i, BLOCK), pl.ds(j, BLOCK)
        stage[c, part, rows, cols] = value.astype(jnp.bfloat16)
        copy = pltpu.make_async_copy(
            stage.at[c, part, rows, cols], out_ref.at[c, part, rows, cols], sems.at[len(copies)]
        )
        copy.start()
        copies.append(copy)

    for c in range(items):
        for r in range(2):
            for a in range(tm_count):
                for b in range(input_count):
                    rows = slice(r * half + a * frames, r * half + (a + 1) * frames)
                    cols = slice(b * inputs, (b + 1) * inputs)
                    held[c, rows, cols] = recv_ref[a, b, c, r]
        turned[c] = held[c].T
        swapped[c, :half] = -held[c, half:]
        swapped[c, half:] = held[c, :half]
        for i in range(0, width, BLOCK):
            for j in range(i, width, BLOCK):
                left = turned[c, i : i + BLOCK]
                real = scale * jnp.dot(
                    left, held[c, :, j : j + BLOCK], preferred_element_type=jnp.float32
                )
                imag = scale * jnp.dot(
                    left, swapped[c, :, j : j + BLOCK], preferred_element_type=jnp.float32
                )
                give(c, 0, i, j, real)
                give(c, 1, i, j, imag)
                if j > i:
                    give(c, 0, j, i, real.T)
                    give(c, 1, j, i, -imag.T)
    for copy in copies:
        copy.wait()


def local(samples, coefficients):
    inputs, sample_count = samples.shape
    taps, fft = coefficients.shape
    frames = sample_count // fft
    tm_count = lax.axis_size("tm")
    input_count = lax.axis_size("input")
    devices = tm_count * input_count
    groups = frames // GROUP
    past = (taps - 1) * fft
    table = jnp.asarray(dft_table(fft))
    vmem = pl.BlockSpec(memory_space=pltpu.VMEM)
    hbm = pl.BlockSpec(memory_space=pltpu.HBM)

    tail = samples[:, sample_count - past :].astype(jnp.bfloat16)
    route = [(i, (i + 1) % tm_count) for i in range(tm_count)]
    halo = lax.ppermute(tail, "tm", route)
    flag = jnp.where(lax.axis_index("tm") > 0, 1.0, 0.0).astype(jnp.float32).reshape(1)

    spectra_type = pltpu.HBM((fft, frames, inputs), jnp.bfloat16)
    in_hbm = lambda array: pltpu.with_memory_space_constraint(array, pltpu.HBM)
    filt = pltpu.VMEM((GROUP, inputs, fft), jnp.bfloat16)
    spread = pltpu.VMEM((fft * GROUP, inputs), jnp.float32)
    spectra, partial = pl.pallas_call(
        own_kernel,
        in_specs=[hbm, hbm, hbm],
        out_specs=[hbm, vmem],
        out_shape=[spectra_type, pltpu.VMEM((GROUP, inputs, fft), jnp.float32)],
        scratch_shapes=[
            pltpu.VMEM((taps, fft), jnp.float32),
            pltpu.VMEM((fft, fft), jnp.bfloat16),
            pltpu.VMEM((groups, inputs, GROUP * fft), jnp.int32),
            filt,
            spread,
            pltpu.VMEM((groups - 1, fft, GROUP, inputs), jnp.bfloat16),
            pltpu.SemaphoreType.DMA((groups + 2,)),
            pltpu.SemaphoreType.DMA((groups - 1,)),
        ],
        compiler_params=pltpu.CompilerParams(vmem_limit_bytes=24 << 20),
        name="own_frames",
    )(in_hbm(samples), in_hbm(coefficients), in_hbm(table))
    spectra = pl.pallas_call(
        first_kernel,
        in_specs=[pl.BlockSpec(memory_space=pltpu.SMEM)] + [vmem] * 4 + [hbm],
        out_specs=hbm,
        out_shape=spectra_type,
        scratch_shapes=[
            filt,
            spread,
            pltpu.VMEM((fft, GROUP, inputs), jnp.bfloat16),
            pltpu.SemaphoreType.DMA,
        ],
        input_output_aliases={5: 0},
        compiler_params=pltpu.CompilerParams(vmem_limit_bytes=16 << 20),
        name="first_frames",
    )(flag, halo, partial, coefficients, table, spectra)

    items = fft // (2 * devices)
    outgoing = spectra.reshape(devices, 2 * items, frames, inputs)
    received = lax.all_to_all(outgoing, ("tm", "input"), 0, 0, tiled=True)
    received = received.reshape(tm_count, input_count, items, 2, frames, inputs)
    depth = 2 * tm_count * frames
    width = input_count * inputs
    blocks = (width // BLOCK) ** 2
    return pl.pallas_call(
        correlate_kernel,
        in_specs=[vmem],
        out_specs=hbm,
        out_shape=jax.ShapeDtypeStruct((items, 2, width, width), jnp.bfloat16),
        scratch_shapes=[
            pltpu.VMEM((items, depth, width), jnp.bfloat16),
            pltpu.VMEM((items, width, depth), jnp.bfloat16),
            pltpu.VMEM((items, depth, width), jnp.bfloat16),
            pltpu.VMEM((items, 2, width, width), jnp.bfloat16),
            pltpu.SemaphoreType.DMA((2 * items * blocks,)),
        ],
        compiler_params=pltpu.CompilerParams(vmem_limit_bytes=36 << 20),
        name="correlate",
    )(received)


def solution(mesh):
    in_specs = (P("input", "tm"), P())
    out_specs = P(("tm", "input"), None, None, None)
    return jax.shard_map(local, mesh=mesh, in_specs=in_specs, out_specs=out_specs, check_vma=False)
```

time: 221 us -> 90.7 us (0.41)
  local copies, waits for them, and re-layouts: 74 us -> 0.01 us
  matrix products: 40.5 us -> 0 us
  other arithmetic: 25.9 us -> 2.53 us
  Pallas kernels: 0 us -> 20.5 us
  blocking collectives: 75.7 us -> 60.8 us
  waiting for transfers between devices: 1.97 us -> 6.68 us
    dot_general x3 -> x0, matrix products: 40.5 us -> none  [the longest x1 26.9 us: local(): jnp.einsum('mn,ifn->mfi', dft_table(fft_length), filtered, preferred_elem...]
    pallas_call x0 -> x3, Pallas kernels: none -> 20.5 us  [the longest x1 9.94 us: local(): pl.pallas_call(own_kernel, in_specs=[hbm, hbm, hbm], out_specs=[hbm, vmem...]
    another operation x2 -> x0, local copies, waits for them, and re-layouts: 18.5 us -> none  [local(): jnp.stack([real_part, imag_part], axis=1)]
    dot_general x2 -> x0, local copies, waits for them, and re-layouts: 18.5 us -> none  [the longest x1 9.75 us: local(): jnp.einsum('tacrfi,tbcrfj->caibj', spectra_block, spectra_block, preferre...]
    convert_element_type x2 -> x0, local copies, waits for them, and re-layouts: 15.6 us -> none  [the longest x1 7.83 us: local(): spectra = jnp.einsum('mn,ifn->mfi', dft_table(fft_length), filtered, pref...]
    all_to_all x1, blocking collectives: 75.7 us -> 60.8 us  [local(): received = lax.all_to_all(outgoing, ('tm', 'input'), 0, 0, tiled=True)]
    sub x1 -> x0, local copies, waits for them, and re-layouts: 13.2 us -> none  [local(): imag_part = cross_part - jnp.transpose(cross_part, (0, 3, 4, 1, 2))]
    sub x1 -> x0, other arithmetic: 11.9 us -> none  [local(): imag_part = cross_part - jnp.transpose(cross_part, (0, 3, 4, 1, 2))]
  transfers between devices with their start and end apart: 1 -> 1, of which waited for: 1 -> 1; matrix products, arithmetic and copies ran while one was open for 0% -> 0% of each run, Pallas kernels for 0% -> 11%
where the time goes in v2:
time: 90.7 us; the launch traced here: 90.5 us
  blocking collectives  60.8 us (67%)
  Pallas kernels  20.5 us (23%)
  waiting for transfers between devices  6.68 us (7%)
  other arithmetic  2.53 us (3%)
    all_to_all x1, blocking collectives, local(): received = lax.all_to_all(outgoing, ('tm', 'input'), 0, 0, tiled=True)  60.8 us
    pallas_call x1, Pallas kernels, local(): pl.pallas_call(own_kernel, in_specs=[hbm, hbm, hbm], out_specs=[hbm, vmem...  9.94 us
    pallas_call x1, Pallas kernels, local(): pl.pallas_call(correlate_kernel, in_specs=[vmem], out_specs=hbm, out_shap...  7.98 us
    ppermute x1, waiting for transfers between devices, local(): halo = lax.ppermute(tail, 'tm', route)  6.68 us
    pallas_call x1, Pallas kernels, local(): pl.pallas_call(first_kernel, in_specs=[pl.BlockSpec(memory_space=pltpu.SM...  2.54 us
    another operation x1, other arithmetic  2.53 us
  transfers between devices with their start and end apart: 1, of which 1 were waited for; matrix products, arithmetic and copies ran while one was open for 0% of the time, Pallas kernels for 11%

profile of v2, /device:TPU:0, one launch (start us, length us, event | category | flops | bytes accessed | tf_op | source)
XLA Modules:
  0.0 90.5 jit_solution(49684634079927706)
XLA Ops:
  0.0 2.5 %slice_convert_fusion = bf16[128,3584]{1,0:T(8,128)(2,1)} fusion(s32[128,16384]{1,0:T(8,128)} %samples_ref.1), kind=kLoop, calls=%fused_computation | loop fusion | flops 458752 | bytes 2752512 | tf_op jit(solution)/shard_map/convert
  2.5 0.0 collective-permute-start
  2.5 0.0 copy-start
  2.5 0.0 copy-start.1
  2.5 9.9 %own_frames.1 = (bf16[512,32,128]{2,1,0:T(8,128)(2,1)}, f32[8,128,512]{2,1,0:T(8,128)S(1)}) custom-call(s32[128,16384]{1,0:T(8,128)} %samples_ref.1, f32[8,512]{1,0:T(8,128)} %coef_ref.1, bf16[512,512]{1,0:T(8,128)(2,1)} %constant.14.clone.table_hbm.table_ref), custom_call_target="tpu_custom_call" | custom-call | tf_op jit(solution)/shard_map/own_frames/pallas_call | solution.py:193
  12.5 6.7 %collective-permute-done.halo_ref = bf16[128,3584]{1,0:T(8,128)(2,1)S(1)} collective-permute-done((bf16[128,3584]{1,0:T(8,128)(2,1)}, bf16[128,3584]{1,0:T(8,128)(2,1)S(1)}, u32[]{:S(2)}, u32[]{:S(2)}) %collective-permute-start) | collective-permute-done | bytes 917536 | tf_op jit(solution)/shard_map/ppermute | solution.py:186
  19.2 0.0 copy-done
  19.2 0.0 copy-done.1
  19.2 2.5 %first_frames.1 = bf16[512,32,128]{2,1,0:T(8,128)(2,1)} custom-call(f32[1]{0:T(128)} %bitcast.flag_ref, bf16[128,3584]{1,0:T(8,128)(2,1)S(1)} %collective-permute-done.halo_ref, f32[8,128,512]{2,1,0:T(8,128)S(1)} %get-tuple-element.7.partial_ref, f32[8,512]{1,0:T(8,128)S(1)} %copy-done.1, ...), custom_call_target="tpu_custom_call", output_to_operand_aliasing={{}: (5, {})} | custom-call | tf_op jit(solution)/shard_map/first_frames/pallas_call | solution.py:211
  21.7 60.8 %all_to_all.5 = bf16[128,4,32,128]{3,2,1,0:T(8,128)(2,1)S(1)} all-to-all(bf16[128,4,32,128]{3,2,1,0:T(8,128)(2,1)} %bitcast.4), channel_id=1, replica_groups=mesh['tm'=16,'input'=8] {'tm','input'}, dimensions={0} | all-to-all | bytes 8388608 | tf_op jit(solution)/shard_map/all_to_all | solution.py:229
  82.5 8.0 %correlate.1 = bf16[2,2,1024,1024]{3,2,1,0:T(8,128)(2,1)} custom-call(bf16[16,8,2,2,32,128]{5,4,3,2,1,0:T(8,128)(2,1)S(1)} %bitcast.3), custom_call_target="tpu_custom_call" | custom-call | tf_op jit(solution)/shard_map/correlate/pallas_call | solution.py:234
Async XLA Ops:
  2.5 16.6 %collective-permute-start = (bf16[128,3584]{1,0:T(8,128)(2,1)}, bf16[128,3584]{1,0:T(8,128)(2,1)S(1)}, u32[]{:S(2)}, u32[]{:S(2)}) collective-permute-start(bf16[128,3584]{1,0:T(8,128)(2,1)} %slice_convert_fusion), channel_id=1, source_target_pairs={{0,8},{8,16},{16,24},{24,32},{32,40},{40,48},{48,56},{56,64},{64,7... | collective-permute-start | bytes 2752520 | tf_op jit(solution)/shard_map/ppermute | solution.py:186
  2.5 16.6 %copy-start = (bf16[512,512]{1,0:T(8,128)(2,1)S(1)}, bf16[512,512]{1,0:T(8,128)(2,1)}, u32[]{:S(2)}) copy-start(bf16[512,512]{1,0:T(8,128)(2,1)} %constant.14.clone.table_hbm.table_ref) | copy-start | bytes 1572868
  2.5 16.6 %copy-start.1 = (f32[8,512]{1,0:T(8,128)S(1)}, f32[8,512]{1,0:T(8,128)}, u32[]{:S(2)}) copy-start(f32[8,512]{1,0:T(8,128)} %coef_ref.1) | copy-start | bytes 49156

commit v3 on v2

--- a/solution.py
+++ b/solution.py
@@ -1,3 +1,5 @@
+import functools
+
 import jax
 import jax.numpy as jnp
 import ml_dtypes
@@ -11,6 +13,7 @@
 BLOCK = 256
 ROWS = 16
 LANES = 128
+AHEAD = 3
 
 
 def dft_table(length):
@@ -20,6 +23,25 @@
     real = (np.arange(length) % 2 == 0)[:, None]
     values = np.where(real, np.cos(angles), -np.sin(angles)) / np.sqrt(length)
     return (values.astype(ml_dtypes.bfloat16).astype(np.float32) / 8.0).astype(ml_dtypes.bfloat16)
+
+
+def edge_frames(frames):
+    return [*range(AHEAD, GROUP), *range(frames, frames + AHEAD)]
+
+
+def tails_kernel(samples_ref, last_ref, first_ref, last, first, sems):
+    count = samples_ref.shape[1]
+    copies = [
+        pltpu.make_async_copy(
+            samples_ref.at[:, pl.ds(count - last.shape[1], last.shape[1])], last, sems.at[0]
+        ),
+        pltpu.make_async_copy(samples_ref.at[:, pl.ds(0, first.shape[1])], first, sems.at[1]),
+    ]
+    for copy in copies:
+        copy.start()
+    for copy, source, target in zip(copies, (last, first), (last_ref, first_ref), strict=True):
+        copy.wait()
+        target[...] = source[...].astype(jnp.float32).astype(jnp.bfloat16)
 
 
 def transform(filt, table_ref, spread, stage, spectra_ref, group, sem):
@@ -46,6 +68,8 @@
 ):
     taps, fft = coef_ref.shape
     groups, inputs, span = held.shape
+    frames = groups * GROUP
+    edge = edge_frames(frames)
     coef_copy = pltpu.make_async_copy(coef_hbm, coef_ref, sems.at[groups])
     coef_copy.start()
     copies = []
@@ -60,8 +84,10 @@
     coef_copy.wait()
     results = []
 
-    for g in range(groups):
-        copies[g].wait()
+    copies[0].wait()
+    for g in [*range(1, groups), 0]:
+        if g:
+            copies[g].wait()
 
         def rows_step(it, carry, g=g):
             rows = pl.ds(pl.multiple_of(it * ROWS, ROWS), ROWS)
@@ -69,21 +95,30 @@
                 coefs = [coef_ref[p : p + 1, n0 : n0 + LANES] for p in range(taps)]
 
                 def frame(f):
-                    where, k = (g, f) if f >= 0 else (g - 1, f + GROUP)
+                    where, k = f // GROUP, f % GROUP
                     return held[where, rows, k * fft + n0 : k * fft + n0 + LANES].astype(jnp.float32)
 
-                window = [frame(f) for f in range(1 - taps, 0)] if g else []
-                for f in range(GROUP):
-                    window.append(frame(f))
-                    total = coefs[0] * window[-1]
-                    for p in range(1, min(taps, len(window))):
-                        total = total + coefs[p] * window[-1 - p]
-                    if g:
-                        filt[f, rows, n0 : n0 + LANES] = total.astype(jnp.bfloat16)
-                    else:
-                        partial_ref[f, rows, n0 : n0 + LANES] = total
-                    if len(window) == taps:
-                        window.pop(0)
+                def share(f, known):
+                    total = None
+                    for p in range(taps):
+                        if f - p in known:
+                            term = coefs[p] * known[f - p]
+                            total = term if total is None else total + term
+                    return total
+
+                if g == 0:
+                    known = {f: frame(f) for f in range(GROUP)}
+                    for slot, f in enumerate(edge[:-AHEAD]):
+                        partial_ref[slot, rows, n0 : n0 + LANES] = share(f, known)
+                    known = {f: frame(f) for f in range(frames + 1 - taps, frames)}
+                    for slot, f in enumerate(edge[-AHEAD:]):
+                        partial_ref[slot + GROUP - AHEAD, rows, n0 : n0 + LANES] = share(f, known)
+                else:
+                    known = {f: frame(f) for f in range(g * GROUP + 1 - taps, g * GROUP)}
+                    for slot in range(GROUP):
+                        f = g * GROUP + slot
+                        known[f] = frame(f)
+                        filt[slot, rows, n0 : n0 + LANES] = share(f, known).astype(jnp.bfloat16)
             return carry
 
         lax.fori_loop(0, inputs // ROWS, rows_step, 0)
@@ -97,27 +132,36 @@
         copy.wait()
 
 
-def first_kernel(
-    flag_ref, halo_ref, partial_ref, coef_ref, table_ref, _, spectra_ref, filt, spread, stage, sem
+def edge_kernel(
+    has_behind_ref, has_own_ref, behind_ref, ahead_ref, partial_ref, coef_ref, table_ref, _, spectra_ref,
+    filt, spread, stage, sem, *, frames,
 ):
     taps, fft = coef_ref.shape
-    inputs = halo_ref.shape[0]
-    past = taps - 1
-    flag = flag_ref[0]
+    inputs = behind_ref.shape[0]
+    past = behind_ref.shape[1] // fft
+    has_behind, has_own = has_behind_ref[0], has_own_ref[0]
 
     def rows_step(it, carry):
         rows = pl.ds(pl.multiple_of(it * ROWS, ROWS), ROWS)
         for n0 in range(0, fft, LANES):
-            coefs = [coef_ref[p : p + 1, n0 : n0 + LANES] * flag for p in range(taps)]
-            window = [
-                halo_ref[rows, k * fft + n0 : k * fft + n0 + LANES].astype(jnp.float32)
-                for k in range(past)
-            ]
-            for f in range(GROUP):
-                total = partial_ref[f, rows, n0 : n0 + LANES]
-                for p in range(f + 1, taps):
-                    total = total + coefs[p] * window[f - p + past]
-                filt[f, rows, n0 : n0 + LANES] = total.astype(jnp.bfloat16)
+            coefs = [coef_ref[p : p + 1, n0 : n0 + LANES] for p in range(taps)]
+            masked = [coef * has_behind for coef in coefs]
+
+            def frame(ref, k):
+                return ref[rows, k * fft + n0 : k * fft + n0 + LANES].astype(jnp.float32)
+
+            behind = [frame(behind_ref, k) for k in range(past)]
+            ahead = [frame(ahead_ref, k) for k in range(AHEAD)]
+            for slot, f in enumerate(edge_frames(frames)):
+                total = partial_ref[slot, rows, n0 : n0 + LANES]
+                if f < frames:
+                    for p in range(f + 1, taps):
+                        total = total + masked[p] * behind[f - p + past]
+                else:
+                    total = total * has_own
+                    for p in range(f - frames + 1):
+                        total = total + coefs[p] * ahead[f - frames - p]
+                filt[slot, rows, n0 : n0 + LANES] = total.astype(jnp.bfloat16)
         return carry
 
     lax.fori_loop(0, inputs // ROWS, rows_step, 0)
@@ -176,20 +220,40 @@
     input_count = lax.axis_size("input")
     devices = tm_count * input_count
     groups = frames // GROUP
-    past = (taps - 1) * fft
+    past = (taps - 1 - AHEAD) * fft
+    ahead = AHEAD * fft
     table = jnp.asarray(dft_table(fft))
     vmem = pl.BlockSpec(memory_space=pltpu.VMEM)
+    smem = pl.BlockSpec(memory_space=pltpu.SMEM)
     hbm = pl.BlockSpec(memory_space=pltpu.HBM)
 
-    tail = samples[:, sample_count - past :].astype(jnp.bfloat16)
-    route = [(i, (i + 1) % tm_count) for i in range(tm_count)]
-    halo = lax.ppermute(tail, "tm", route)
-    flag = jnp.where(lax.axis_index("tm") > 0, 1.0, 0.0).astype(jnp.float32).reshape(1)
-
+    ring = [(i, (i + 1) % tm_count) for i in range(tm_count)]
+    own_tm = lax.axis_index("tm")
+    has_behind = jnp.where(own_tm > 0, 1.0, 0.0).astype(jnp.float32).reshape(1)
+    has_own = jnp.where(own_tm < tm_count - 1, 1.0, 0.0).astype(jnp.float32).reshape(1)
     spectra_type = pltpu.HBM((fft, frames, inputs), jnp.bfloat16)
     in_hbm = lambda array: pltpu.with_memory_space_constraint(array, pltpu.HBM)
     filt = pltpu.VMEM((GROUP, inputs, fft), jnp.bfloat16)
     spread = pltpu.VMEM((fft * GROUP, inputs), jnp.float32)
+    last, first = pl.pallas_call(
+        tails_kernel,
+        in_specs=[hbm],
+        out_specs=[vmem, vmem],
+        out_shape=[
+            pltpu.VMEM((inputs, past), jnp.bfloat16),
+            pltpu.VMEM((inputs, ahead), jnp.bfloat16),
+        ],
+        scratch_shapes=[
+            pltpu.VMEM((inputs, past), jnp.int32),
+            pltpu.VMEM((inputs, ahead), jnp.int32),
+            pltpu.SemaphoreType.DMA((2,)),
+        ],
+        compiler_params=pltpu.CompilerParams(vmem_limit_bytes=8 << 20),
+        name="tails",
+    )(in_hbm(samples))
+    from_behind = lax.ppermute(last, "tm", ring)
+    from_ahead = lax.ppermute(first, "tm", [(b, a) for a, b in ring])
+
     spectra, partial = pl.pallas_call(
         own_kernel,
         in_specs=[hbm, hbm, hbm],
@@ -209,8 +273,8 @@
         name="own_frames",
     )(in_hbm(samples), in_hbm(coefficients), in_hbm(table))
     spectra = pl.pallas_call(
-        first_kernel,
-        in_specs=[pl.BlockSpec(memory_space=pltpu.SMEM)] + [vmem] * 4 + [hbm],
+        functools.partial(edge_kernel, frames=frames),
+        in_specs=[smem] * 2 + [vmem] * 5 + [hbm],
         out_specs=hbm,
         out_shape=spectra_type,
         scratch_shapes=[
@@ -219,10 +283,10 @@
             pltpu.VMEM((fft, GROUP, inputs), jnp.bfloat16),
             pltpu.SemaphoreType.DMA,
         ],
-        input_output_aliases={5: 0},
+        input_output_aliases={7: 0},
         compiler_params=pltpu.CompilerParams(vmem_limit_bytes=16 << 20),
-        name="first_frames",
-    )(flag, halo, partial, coefficients, table, spectra)
+        name="edge_frames",
+    )(has_behind, has_own, from_behind, from_ahead, partial, coefficients, table, spectra)
 
     items = fft // (2 * devices)
     outgoing = spectra.reshape(devices, 2 * items, frames, inputs)

time: 90.7 us -> 88.2 us (0.972)
  waiting for transfers between devices: 6.68 us -> 0.01 us
  starting transfers between devices: 0.01 us -> 5.42 us
  other arithmetic: 2.53 us -> 0 us
  Pallas kernels: 20.5 us -> 21.8 us
    ppermute x1 -> x2, waiting for transfers between devices: 6.68 us -> 0.01 us  [the longest x1 0.01 us: local(): from_behind = lax.ppermute(last, 'tm', ring)]
    ppermute x1 -> x2, starting transfers between devices: 0.01 us -> 5.42 us  [the longest x1 5.35 us: local(): from_ahead = lax.ppermute(first, 'tm', [(b, a) for a, b in ring])]
    another operation x1 -> x0, other arithmetic: 2.53 us -> none
    pallas_call x1 -> x2, Pallas kernels: 2.54 us -> 3.87 us  [the longest x1 2.36 us: local(): pl.pallas_call(functools.partial(edge_kernel, frames=frames), in_specs=[s...]
  transfers between devices with their start and end apart: 1 -> 2, of which waited for: 1 -> 0; matrix products, arithmetic and copies ran while one was open for 0% -> 0% of each run, Pallas kernels for 11% -> 11%
where the time goes in v3:
time: 88.2 us; the launch traced here: 88 us
  blocking collectives  60.8 us (69%)
  Pallas kernels  21.8 us (25%)
  starting transfers between devices  5.42 us (6%)
    all_to_all x1, blocking collectives, local(): received = lax.all_to_all(outgoing, ('tm', 'input'), 0, 0, tiled=True)  60.8 us
    pallas_call x1, Pallas kernels, local(): pl.pallas_call(own_kernel, in_specs=[hbm, hbm, hbm], out_specs=[hbm, vmem...  9.9 us
    pallas_call x1, Pallas kernels, local(): pl.pallas_call(correlate_kernel, in_specs=[vmem], out_specs=hbm, out_shap...  7.98 us
    ppermute x1, starting transfers between devices, local(): from_ahead = lax.ppermute(first, 'tm', [(b, a) for a, b in ring])  5.35 us
    pallas_call x1, Pallas kernels, local(): pl.pallas_call(functools.partial(edge_kernel, frames=frames), in_specs=[s...  2.36 us
  transfers between devices with their start and end apart: 2, of which 0 were waited for; matrix products, arithmetic and copies ran while one was open for 0% of the time, Pallas kernels for 11%

profile of v3, /device:TPU:0, one launch (start us, length us, event | category | flops | bytes accessed | tf_op | source)
XLA Modules:
  0.0 88.0 jit_solution(2802929977713165936)
XLA Ops:
  0.0 1.5 %tails.1 = (bf16[128,2048]{1,0:T(8,128)(2,1)S(1)}, bf16[128,1536]{1,0:T(8,128)(2,1)S(1)}) custom-call(s32[128,16384]{1,0:T(8,128)} %samples_ref.3), custom_call_target="tpu_custom_call" | custom-call | tf_op jit(solution)/shard_map/tails/pallas_call | solution.py:238
  1.5 0.1 collective-permute-start
  1.6 5.3 %collective-permute-start.1 = (bf16[128,1536]{1,0:T(8,128)(2,1)S(1)}, bf16[128,1536]{1,0:T(8,128)(2,1)S(1)}, u32[]{:S(2)}, u32[]{:S(2)}) collective-permute-start(bf16[128,1536]{1,0:T(8,128)(2,1)S(1)} %get-tuple-element.10), channel_id=1, source_target_pairs={{8,0},{16,8},{24,16},{32,24},{40,32},{48,40},{56,48},{64,56},{72,6... | collective-permute-start | bytes 1179656 | tf_op jit(solution)/shard_map/ppermute | solution.py:255
  6.9 0.0 copy-start
  6.9 0.0 copy-start.1
  6.9 9.9 %own_frames.1 = (bf16[512,32,128]{2,1,0:T(8,128)(2,1)}, f32[8,128,512]{2,1,0:T(8,128)S(1)}) custom-call(s32[128,16384]{1,0:T(8,128)} %samples_ref.3, f32[8,512]{1,0:T(8,128)} %coef_ref.1, bf16[512,512]{1,0:T(8,128)(2,1)} %constant.16.clone.table_hbm.table_ref), custom_call_target="tpu_custom_call" | custom-call | tf_op jit(solution)/shard_map/own_frames/pallas_call | solution.py:257
  16.9 0.0 collective-permute-done.1.ahead_ref
  16.9 0.0 collective-permute-done.behind_ref
  16.9 0.0 copy-done
  16.9 0.0 copy-done.1
  16.9 2.4 %edge_frames.1 = bf16[512,32,128]{2,1,0:T(8,128)(2,1)} custom-call(f32[1]{0:T(128)} %bitcast.has_behind_ref, f32[1]{0:T(128)} %bitcast.1.has_own_ref, bf16[128,2048]{1,0:T(8,128)(2,1)S(1)} %collective-permute-done.behind_ref, bf16[128,1536]{1,0:T(8,128)(2,1)S(1)} %collective-permute-done.1.ahead_ref, ...), custom_call_target="tpu_custom_call", output_to_operand_aliasing={{}: (7, {})} | custom-call | tf_op jit(solution)/shard_map/edge_frames/pallas_call | solution.py:275
  19.3 60.8 %all_to_all.5 = bf16[128,4,32,128]{3,2,1,0:T(8,128)(2,1)S(1)} all-to-all(bf16[128,4,32,128]{3,2,1,0:T(8,128)(2,1)} %bitcast.5), channel_id=1, replica_groups=mesh['tm'=16,'input'=8] {'tm','input'}, dimensions={0} | all-to-all | bytes 8388608 | tf_op jit(solution)/shard_map/all_to_all | solution.py:293
  80.0 8.0 %correlate.1 = bf16[2,2,1024,1024]{3,2,1,0:T(8,128)(2,1)} custom-call(bf16[16,8,2,2,32,128]{5,4,3,2,1,0:T(8,128)(2,1)S(1)} %bitcast.4), custom_call_target="tpu_custom_call" | custom-call | tf_op jit(solution)/shard_map/correlate/pallas_call | solution.py:298
Async XLA Ops:
  1.5 15.4 %collective-permute-start = (bf16[128,2048]{1,0:T(8,128)(2,1)S(1)}, bf16[128,2048]{1,0:T(8,128)(2,1)S(1)}, u32[]{:S(2)}, u32[]{:S(2)}) collective-permute-start(bf16[128,2048]{1,0:T(8,128)(2,1)S(1)} %get-tuple-element.9), channel_id=1, source_target_pairs={{0,8},{8,16},{16,24},{24,32},{32,40},{40,48},{48,56},{56,64},{64,7... | collective-permute-start | bytes 1572872 | tf_op jit(solution)/shard_map/ppermute | solution.py:254
  1.6 15.3 %collective-permute-start.1 = (bf16[128,1536]{1,0:T(8,128)(2,1)S(1)}, bf16[128,1536]{1,0:T(8,128)(2,1)S(1)}, u32[]{:S(2)}, u32[]{:S(2)}) collective-permute-start(bf16[128,1536]{1,0:T(8,128)(2,1)S(1)} %get-tuple-element.10), channel_id=1, source_target_pairs={{8,0},{16,8},{24,16},{32,24},{40,32},{48,40},{56,48},{64,56},{72,6... | collective-permute-start | bytes 1179656 | tf_op jit(solution)/shard_map/ppermute | solution.py:255
  6.9 9.9 %copy-start = (bf16[512,512]{1,0:T(8,128)(2,1)S(1)}, bf16[512,512]{1,0:T(8,128)(2,1)}, u32[]{:S(2)}) copy-start(bf16[512,512]{1,0:T(8,128)(2,1)} %constant.16.clone.table_hbm.table_ref) | copy-start | bytes 1572868
  6.9 9.9 %copy-start.1 = (f32[8,512]{1,0:T(8,128)S(1)}, f32[8,512]{1,0:T(8,128)}, u32[]{:S(2)}) copy-start(f32[8,512]{1,0:T(8,128)} %coef_ref.1) | copy-start | bytes 49156

commit v4 on v3

--- a/solution.py
+++ b/solution.py
@@ -16,13 +16,40 @@
 AHEAD = 3
 
 
-def dft_table(length):
-    channel = np.arange(length) // 2
-    phase = channel[:, None] * np.arange(length)[None, :] % length
+def half_tables(length, items):
+    assert items == 2
+    channel = np.arange(length // 2).reshape(-1, items).T
+    phase = channel[:, :, None] * np.arange(length // 2) % length
     angles = phase * (2.0 * np.pi / length)
-    real = (np.arange(length) % 2 == 0)[:, None]
-    values = np.where(real, np.cos(angles), -np.sin(angles)) / np.sqrt(length)
-    return (values.astype(ml_dtypes.bfloat16).astype(np.float32) / 8.0).astype(ml_dtypes.bfloat16)
+    values = np.stack([np.cos(angles), -np.sin(angles)], axis=1) / np.sqrt(length)
+    values = values.astype(ml_dtypes.bfloat16).astype(np.float32) / 8.0
+    return values.reshape(items, -1, length // 2).astype(ml_dtypes.bfloat16)
+
+
+def transform(filt, h, f, table_ref, spread):
+    _, frames, inputs, half = filt.shape
+    pair = filt[h, pl.ds(f, 2)].reshape(2 * inputs, half)
+    spectra = lax.dot_general(
+        table_ref[h], pair, (((1,), (1,)), ((), ())), preferred_element_type=jnp.float32
+    )
+    devices = half // 2
+    stride = 4 * frames
+    for r in range(2):
+        rows = spectra[r * devices : (r + 1) * devices]
+        first = (2 * h + r) * frames + f
+        spread[pl.ds(first, devices, stride=stride), :] = rows[:, :inputs]
+        spread[pl.ds(first + 1, devices, stride=stride), :] = rows[:, inputs:]
+
+
+def pack(spread, stage, part, parts):
+    rows, frames, inputs = stage.shape
+    count = rows // parts
+    block = spread[pl.ds(part * count * frames, count * frames), :]
+    stage[pl.ds(part * count, count)] = block.reshape(count, frames, inputs).astype(jnp.bfloat16)
+
+
+def halves(low, high):
+    return (low + high).astype(jnp.bfloat16), (low - high).astype(jnp.bfloat16)
 
 
 def edge_frames(frames):
@@ -44,32 +71,16 @@
         target[...] = source[...].astype(jnp.float32).astype(jnp.bfloat16)
 
 
-def transform(filt, table_ref, spread, stage, spectra_ref, group, sem):
-    frames, inputs, fft = filt.shape
-    for f in range(0, frames, 2):
-        pair = filt[f : f + 2].reshape(2 * inputs, fft)
-        spectra = lax.dot_general(
-            table_ref[...], pair, (((1,), (1,)), ((), ())), preferred_element_type=jnp.float32
-        )
-        spread[pl.ds(f, fft, stride=frames), :] = spectra[:, :inputs]
-        spread[pl.ds(f + 1, fft, stride=frames), :] = spectra[:, inputs:]
-    block = spread[...].reshape(fft, frames, inputs).astype(jnp.bfloat16)
-    stage[...] = block
-    copy = pltpu.make_async_copy(
-        stage, spectra_ref.at[:, pl.ds(group * frames, frames), :], sem
-    )
-    copy.start()
-    return copy
-
-
 def own_kernel(
     samples_ref, coef_hbm, table_hbm, spectra_ref, partial_ref,
-    coef_ref, table_ref, held, filt, spread, stage, sems, out_sems,
+    coef_ref, table_ref, held, filts, spreads, stage, sems, out_sems,
 ):
     taps, fft = coef_ref.shape
     groups, inputs, span = held.shape
     frames = groups * GROUP
+    half = fft // 2
     edge = edge_frames(frames)
+    steps = inputs // ROWS
     coef_copy = pltpu.make_async_copy(coef_hbm, coef_ref, sems.at[groups])
     coef_copy.start()
     copies = []
@@ -82,90 +93,132 @@
     table_copy = pltpu.make_async_copy(table_hbm, table_ref, sems.at[groups + 1])
     table_copy.start()
     coef_copy.wait()
+
+    def filter_rows(g, it):
+        rows = pl.ds(pl.multiple_of(it * ROWS, ROWS), ROWS)
+
+        def frame(f, n):
+            where, k = f // GROUP, f % GROUP
+            return held[where, rows, k * fft + n : k * fft + n + LANES].astype(jnp.float32)
+
+        def share(f, known, n):
+            total = None
+            for p in range(taps):
+                if f - p in known:
+                    term = coef_ref[p : p + 1, n : n + LANES] * known[f - p]
+                    total = term if total is None else total + term
+            return total
+
+        if g == 0:
+            for n in range(0, fft, LANES):
+                known = {f: frame(f, n) for f in range(GROUP)}
+                for slot, f in enumerate(edge[:-AHEAD]):
+                    partial_ref[slot, rows, n : n + LANES] = share(f, known, n)
+                known = {f: frame(f, n) for f in range(frames + 1 - taps, frames)}
+                for slot, f in enumerate(edge[-AHEAD:]):
+                    partial_ref[slot + GROUP - AHEAD, rows, n : n + LANES] = share(f, known, n)
+            return
+        filt = filts[g % 2]
+        for n in range(0, half, LANES):
+            known = [
+                {f: frame(f, n + m) for f in range(g * GROUP + 1 - taps, g * GROUP)} for m in (0, half)
+            ]
+            for slot in range(GROUP):
+                f = g * GROUP + slot
+                totals = []
+                for m, seen in zip((0, half), known, strict=True):
+                    seen[f] = frame(f, n + m)
+                    totals.append(share(f, seen, n + m))
+                even, odd = halves(*totals)
+                filt[0, slot, rows, n : n + LANES] = even
+                filt[1, slot, rows, n : n + LANES] = odd
+
     results = []
 
+    def send(g):
+        copy = pltpu.make_async_copy(
+            stage.at[g - 1], spectra_ref.at[:, pl.ds(g * GROUP, GROUP), :], out_sems.at[g - 1]
+        )
+        copy.start()
+        results.append(copy)
+
     copies[0].wait()
-    for g in [*range(1, groups), 0]:
+    order = [*range(1, groups), 0]
+    for at, g in enumerate(order):
         if g:
             copies[g].wait()
-
-        def rows_step(it, carry, g=g):
-            rows = pl.ds(pl.multiple_of(it * ROWS, ROWS), ROWS)
-            for n0 in range(0, fft, LANES):
-                coefs = [coef_ref[p : p + 1, n0 : n0 + LANES] for p in range(taps)]
-
-                def frame(f):
-                    where, k = f // GROUP, f % GROUP
-                    return held[where, rows, k * fft + n0 : k * fft + n0 + LANES].astype(jnp.float32)
-
-                def share(f, known):
-                    total = None
-                    for p in range(taps):
-                        if f - p in known:
-                            term = coefs[p] * known[f - p]
-                            total = term if total is None else total + term
-                    return total
-
-                if g == 0:
-                    known = {f: frame(f) for f in range(GROUP)}
-                    for slot, f in enumerate(edge[:-AHEAD]):
-                        partial_ref[slot, rows, n0 : n0 + LANES] = share(f, known)
-                    known = {f: frame(f) for f in range(frames + 1 - taps, frames)}
-                    for slot, f in enumerate(edge[-AHEAD:]):
-                        partial_ref[slot + GROUP - AHEAD, rows, n0 : n0 + LANES] = share(f, known)
-                else:
-                    known = {f: frame(f) for f in range(g * GROUP + 1 - taps, g * GROUP)}
-                    for slot in range(GROUP):
-                        f = g * GROUP + slot
-                        known[f] = frame(f)
-                        filt[slot, rows, n0 : n0 + LANES] = share(f, known).astype(jnp.bfloat16)
+        if at == 1:
+            table_copy.wait()
+        if at >= 3:
+            send(order[at - 3])
+
+        def step(it, carry, at=at, g=g):
+            if at >= 1:
+                last = order[at - 1]
+                transform(filts[last % 2], it % 2, it // 2 * 2, table_ref, spreads[last % 2])
+            if at >= 2:
+                before = order[at - 2]
+                pack(spreads[before % 2], stage.at[before - 1], it, steps)
+            filter_rows(g, it)
             return carry
 
-        lax.fori_loop(0, inputs // ROWS, rows_step, 0)
-        if g:
-            if g == 1:
-                table_copy.wait()
-            results.append(
-                transform(filt, table_ref, spread, stage.at[g - 1], spectra_ref, g, out_sems.at[g - 1])
-            )
+        lax.fori_loop(0, steps, step, 0)
+    send(order[-3])
+    pack(spreads[order[-2] % 2], stage.at[order[-2] - 1], 0, 1)
+    send(order[-2])
     for copy in results:
         copy.wait()
 
 
 def edge_kernel(
     has_behind_ref, has_own_ref, behind_ref, ahead_ref, partial_ref, coef_ref, table_ref, _, spectra_ref,
-    filt, spread, stage, sem, *, frames,
+    filt, spread, stage, sems, *, frames,
 ):
     taps, fft = coef_ref.shape
+    half = fft // 2
     inputs = behind_ref.shape[0]
     past = behind_ref.shape[1] // fft
     has_behind, has_own = has_behind_ref[0], has_own_ref[0]
-
-    def rows_step(it, carry):
-        rows = pl.ds(pl.multiple_of(it * ROWS, ROWS), ROWS)
-        for n0 in range(0, fft, LANES):
-            coefs = [coef_ref[p : p + 1, n0 : n0 + LANES] for p in range(taps)]
-            masked = [coef * has_behind for coef in coefs]
-
-            def frame(ref, k):
-                return ref[rows, k * fft + n0 : k * fft + n0 + LANES].astype(jnp.float32)
-
-            behind = [frame(behind_ref, k) for k in range(past)]
-            ahead = [frame(ahead_ref, k) for k in range(AHEAD)]
-            for slot, f in enumerate(edge_frames(frames)):
-                total = partial_ref[slot, rows, n0 : n0 + LANES]
-                if f < frames:
-                    for p in range(f + 1, taps):
-                        total = total + masked[p] * behind[f - p + past]
-                else:
-                    total = total * has_own
-                    for p in range(f - frames + 1):
-                        total = total + coefs[p] * ahead[f - frames - p]
-                filt[slot, rows, n0 : n0 + LANES] = total.astype(jnp.bfloat16)
-        return carry
-
-    lax.fori_loop(0, inputs // ROWS, rows_step, 0)
-    transform(filt, table_ref, spread, stage, spectra_ref, 0, sem).wait()
+    edge = edge_frames(frames)
+
+    def total(slot, rows, n):
+        f = edge[slot]
+        value = partial_ref[slot, rows, n : n + LANES]
+        if f < frames:
+            for p in range(f + 1, taps):
+                k = f - p + past
+                sample = behind_ref[rows, k * fft + n : k * fft + n + LANES].astype(jnp.float32)
+                value = value + (coef_ref[p : p + 1, n : n + LANES] * has_behind) * sample
+        else:
+            value = value * has_own
+            for p in range(f - frames + 1):
+                k = f - frames - p
+                sample = ahead_ref[rows, k * fft + n : k * fft + n + LANES].astype(jnp.float32)
+                value = value + coef_ref[p : p + 1, n : n + LANES] * sample
+        return value
+
+    for slot in range(0, GROUP, 2):
+        for i in range(0, inputs, ROWS):
+            rows = slice(i, i + ROWS)
+            for n in range(0, half, LANES):
+                for s in (slot, slot + 1):
+                    even, odd = halves(total(s, rows, n), total(s, rows, n + half))
+                    filt[0, s, rows, n : n + LANES] = even
+                    filt[1, s, rows, n : n + LANES] = odd
+        for h in range(2):
+            transform(filt, h, slot, table_ref, spread)
+    parts = sems.shape[0]
+    copies = []
+    for part in range(parts):
+        pack(spread, stage, part, parts)
+        rows = pl.ds(part * (fft // parts), fft // parts)
+        copy = pltpu.make_async_copy(
+            stage.at[rows], spectra_ref.at[rows, pl.ds(0, GROUP), :], sems.at[part]
+        )
+        copy.start()
+        copies.append(copy)
+    for copy in copies:
+        copy.wait()
 
 
 def correlate_kernel(recv_ref, out_ref, held, turned, swapped, stage, sems):
@@ -222,7 +275,8 @@
     groups = frames // GROUP
     past = (taps - 1 - AHEAD) * fft
     ahead = AHEAD * fft
-    table = jnp.asarray(dft_table(fft))
+    items = fft // (2 * devices)
+    table = jnp.asarray(half_tables(fft, items))
     vmem = pl.BlockSpec(memory_space=pltpu.VMEM)
     smem = pl.BlockSpec(memory_space=pltpu.SMEM)
     hbm = pl.BlockSpec(memory_space=pltpu.HBM)
@@ -233,7 +287,7 @@
     has_own = jnp.where(own_tm < tm_count - 1, 1.0, 0.0).astype(jnp.float32).reshape(1)
     spectra_type = pltpu.HBM((fft, frames, inputs), jnp.bfloat16)
     in_hbm = lambda array: pltpu.with_memory_space_constraint(array, pltpu.HBM)
-    filt = pltpu.VMEM((GROUP, inputs, fft), jnp.bfloat16)
+    filt = pltpu.VMEM((2, GROUP, inputs, fft // 2), jnp.bfloat16)
     spread = pltpu.VMEM((fft * GROUP, inputs), jnp.float32)
     last, first = pl.pallas_call(
         tails_kernel,
@@ -261,10 +315,10 @@
         out_shape=[spectra_type, pltpu.VMEM((GROUP, inputs, fft), jnp.float32)],
         scratch_shapes=[
             pltpu.VMEM((taps, fft), jnp.float32),
-            pltpu.VMEM((fft, fft), jnp.bfloat16),
+            pltpu.VMEM(table.shape, jnp.bfloat16),
             pltpu.VMEM((groups, inputs, GROUP * fft), jnp.int32),
-            filt,
-            spread,
+            [filt, filt],
+            [spread, spread],
             pltpu.VMEM((groups - 1, fft, GROUP, inputs), jnp.bfloat16),
             pltpu.SemaphoreType.DMA((groups + 2,)),
             pltpu.SemaphoreType.DMA((groups - 1,)),
@@ -281,14 +335,13 @@
             filt,
             spread,
             pltpu.VMEM((fft, GROUP, inputs), jnp.bfloat16),
-            pltpu.SemaphoreType.DMA,
+            pltpu.SemaphoreType.DMA((4,)),
         ],
         input_output_aliases={7: 0},
         compiler_params=pltpu.CompilerParams(vmem_limit_bytes=16 << 20),
         name="edge_frames",
     )(has_behind, has_own, from_behind, from_ahead, partial, coefficients, table, spectra)
 
-    items = fft // (2 * devices)
     outgoing = spectra.reshape(devices, 2 * items, frames, inputs)
     received = lax.all_to_all(outgoing, ("tm", "input"), 0, 0, tiled=True)
     received = received.reshape(tm_count, input_count, items, 2, frames, inputs)

time: 88.2 us -> 92.4 us (1.048)
  Pallas kernels: 21.8 us -> 25.9 us
    pallas_call x1, Pallas kernels: 9.9 us -> 13.6 us  [local(): pl.pallas_call(own_kernel, in_specs=[hbm, hbm, hbm], out_specs=[hbm, vmem...]
  transfers between devices with their start and end apart: 2 -> 2, of which waited for: 0 -> 0; matrix products, arithmetic and copies ran while one was open for 0% -> 0% of each run, Pallas kernels for 11% -> 15%
where the time goes in v4:
time: 92.4 us; the launch traced here: 92.2 us
  blocking collectives  60.8 us (66%)
  Pallas kernels  25.9 us (28%)
  starting transfers between devices  5.42 us (6%)
    all_to_all x1, blocking collectives, local(): received = lax.all_to_all(outgoing, ('tm', 'input'), 0, 0, tiled=True)  60.8 us
    pallas_call x1, Pallas kernels, local(): pl.pallas_call(own_kernel, in_specs=[hbm, hbm, hbm], out_specs=[hbm, vmem...  13.6 us
    pallas_call x1, Pallas kernels, local(): pl.pallas_call(correlate_kernel, in_specs=[vmem], out_specs=hbm, out_shap...  8 us
    ppermute x1, starting transfers between devices, local(): from_ahead = lax.ppermute(first, 'tm', [(b, a) for a, b in ring])  5.35 us
    pallas_call x1, Pallas kernels, local(): pl.pallas_call(functools.partial(edge_kernel, frames=frames), in_specs=[s...  2.83 us
  transfers between devices with their start and end apart: 2, of which 0 were waited for; matrix products, arithmetic and copies ran while one was open for 0% of the time, Pallas kernels for 15%

profile of v4, /device:TPU:0, one launch (start us, length us, event | category | flops | bytes accessed | tf_op | source)
XLA Modules:
  0.0 92.2 jit_solution(6427303327032472664)
XLA Ops:
  0.0 1.5 %tails.1 = (bf16[128,2048]{1,0:T(8,128)(2,1)S(1)}, bf16[128,1536]{1,0:T(8,128)(2,1)S(1)}) custom-call(s32[128,16384]{1,0:T(8,128)} %samples_ref.3), custom_call_target="tpu_custom_call" | custom-call | tf_op jit(solution)/shard_map/tails/pallas_call | solution.py:292
  1.5 0.1 collective-permute-start
  1.6 5.3 %collective-permute-start.1 = (bf16[128,1536]{1,0:T(8,128)(2,1)S(1)}, bf16[128,1536]{1,0:T(8,128)(2,1)S(1)}, u32[]{:S(2)}, u32[]{:S(2)}) collective-permute-start(bf16[128,1536]{1,0:T(8,128)(2,1)S(1)} %get-tuple-element.10), channel_id=1, source_target_pairs={{8,0},{16,8},{24,16},{32,24},{40,32},{48,40},{56,48},{64,56},{72,6... | collective-permute-start | bytes 1179656 | tf_op jit(solution)/shard_map/ppermute | solution.py:309
  6.9 0.0 copy-start
  6.9 0.0 copy-start.1
  6.9 13.6 %own_frames.1 = (bf16[512,32,128]{2,1,0:T(8,128)(2,1)}, f32[8,128,512]{2,1,0:T(8,128)S(1)}) custom-call(s32[128,16384]{1,0:T(8,128)} %samples_ref.3, f32[8,512]{1,0:T(8,128)} %coef_ref.1, bf16[2,256,256]{2,1,0:T(8,128)(2,1)} %constant.16.clone.table_hbm.table_ref), custom_call_target="tpu_custom_call" | custom-call | tf_op jit(solution)/shard_map/own_frames/pallas_call | solution.py:311
  20.6 0.0 collective-permute-done.1.ahead_ref
  20.6 0.0 collective-permute-done.behind_ref
  20.6 0.0 copy-done
  20.6 0.0 copy-done.1
  20.6 2.8 %edge_frames.1 = bf16[512,32,128]{2,1,0:T(8,128)(2,1)} custom-call(f32[1]{0:T(128)} %bitcast.has_behind_ref, f32[1]{0:T(128)} %bitcast.1.has_own_ref, bf16[128,2048]{1,0:T(8,128)(2,1)S(1)} %collective-permute-done.behind_ref, bf16[128,1536]{1,0:T(8,128)(2,1)S(1)} %collective-permute-done.1.ahead_ref, ...), custom_call_target="tpu_custom_call", output_to_operand_aliasing={{}: (7, {})} | custom-call | tf_op jit(solution)/shard_map/edge_frames/pallas_call | solution.py:329
  23.4 60.8 %all_to_all.5 = bf16[128,4,32,128]{3,2,1,0:T(8,128)(2,1)S(1)} all-to-all(bf16[128,4,32,128]{3,2,1,0:T(8,128)(2,1)} %bitcast.5), channel_id=1, replica_groups=mesh['tm'=16,'input'=8] {'tm','input'}, dimensions={0} | all-to-all | bytes 8388608 | tf_op jit(solution)/shard_map/all_to_all | solution.py:346
  84.2 8.0 %correlate.1 = bf16[2,2,1024,1024]{3,2,1,0:T(8,128)(2,1)} custom-call(bf16[16,8,2,2,32,128]{5,4,3,2,1,0:T(8,128)(2,1)S(1)} %bitcast.4), custom_call_target="tpu_custom_call" | custom-call | tf_op jit(solution)/shard_map/correlate/pallas_call | solution.py:351
Async XLA Ops:
  1.5 19.1 %collective-permute-start = (bf16[128,2048]{1,0:T(8,128)(2,1)S(1)}, bf16[128,2048]{1,0:T(8,128)(2,1)S(1)}, u32[]{:S(2)}, u32[]{:S(2)}) collective-permute-start(bf16[128,2048]{1,0:T(8,128)(2,1)S(1)} %get-tuple-element.9), channel_id=1, source_target_pairs={{0,8},{8,16},{16,24},{24,32},{32,40},{40,48},{48,56},{56,64},{64,7... | collective-permute-start | bytes 1572872 | tf_op jit(solution)/shard_map/ppermute | solution.py:308
  1.6 19.0 %collective-permute-start.1 = (bf16[128,1536]{1,0:T(8,128)(2,1)S(1)}, bf16[128,1536]{1,0:T(8,128)(2,1)S(1)}, u32[]{:S(2)}, u32[]{:S(2)}) collective-permute-start(bf16[128,1536]{1,0:T(8,128)(2,1)S(1)} %get-tuple-element.10), channel_id=1, source_target_pairs={{8,0},{16,8},{24,16},{32,24},{40,32},{48,40},{56,48},{64,56},{72,6... | collective-permute-start | bytes 1179656 | tf_op jit(solution)/shard_map/ppermute | solution.py:309
  6.9 13.6 %copy-start = (bf16[2,256,256]{2,1,0:T(8,128)(2,1)S(1)}, bf16[2,256,256]{2,1,0:T(8,128)(2,1)}, u32[]{:S(2)}) copy-start(bf16[2,256,256]{2,1,0:T(8,128)(2,1)} %constant.16.clone.table_hbm.table_ref) | copy-start | bytes 786436
  6.9 13.7 %copy-start.1 = (f32[8,512]{1,0:T(8,128)S(1)}, f32[8,512]{1,0:T(8,128)}, u32[]{:S(2)}) copy-start(f32[8,512]{1,0:T(8,128)} %coef_ref.1) | copy-start | bytes 49156

commit v5 on v4

v5 whole, which is shorter than its diff:
```python
import functools

import jax
import jax.numpy as jnp
import ml_dtypes
import numpy as np
from jax import lax
from jax.experimental import pallas as pl
from jax.experimental.pallas import tpu as pltpu
from jax.sharding import PartitionSpec as P

GROUP = 8
BLOCK = 256
ROWS = 16
LANES = 128
AHEAD = 3


def dft_table(length):
    channel = np.arange(length) // 2
    phase = channel[:, None] * np.arange(length)[None, :] % length
    angles = phase * (2.0 * np.pi / length)
    real = (np.arange(length) % 2 == 0)[:, None]
    values = np.where(real, np.cos(angles), -np.sin(angles)) / np.sqrt(length)
    return (values.astype(ml_dtypes.bfloat16).astype(np.float32) / 8.0).astype(ml_dtypes.bfloat16)


def edge_frames(frames):
    return [*range(AHEAD, GROUP), *range(frames, frames + AHEAD)]


def tails_kernel(samples_ref, last_ref, first_ref, last, first, sems):
    count = samples_ref.shape[1]
    copies = [
        pltpu.make_async_copy(
            samples_ref.at[:, pl.ds(count - last.shape[1], last.shape[1])], last, sems.at[0]
        ),
        pltpu.make_async_copy(samples_ref.at[:, pl.ds(0, first.shape[1])], first, sems.at[1]),
    ]
    for copy in copies:
        copy.start()
    for copy, source, target in zip(copies, (last, first), (last_ref, first_ref), strict=True):
        copy.wait()
        target[...] = source[...].astype(jnp.float32).astype(jnp.bfloat16)


def transform_pair(filt, f, table_ref, spread):
    frames, inputs, fft = filt.shape
    pair = filt[f : f + 2].reshape(2 * inputs, fft)
    spectra = lax.dot_general(
        table_ref[...], pair, (((1,), (1,)), ((), ())), preferred_element_type=jnp.float32
    )
    spread[pl.ds(f, fft, stride=frames), :] = spectra[:, :inputs]
    spread[pl.ds(f + 1, fft, stride=frames), :] = spectra[:, inputs:]


def pack(spread, stage, part, parts):
    rows, frames, inputs = stage.shape
    count = rows // parts
    block = spread[part * count * frames : (part + 1) * count * frames, :]
    stage[part * count : (part + 1) * count] = block.reshape(count, frames, inputs).astype(
        jnp.bfloat16
    )


def own_kernel(
    samples_ref, coef_hbm, table_hbm, spectra_ref, partial_ref,
    coef_ref, table_ref, held, filts, spreads, stage, sems, out_sems,
):
    taps, fft = coef_ref.shape
    groups, inputs, span = held.shape
    frames = groups * GROUP
    edge = edge_frames(frames)

    def load(g):
        copy = pltpu.make_async_copy(
            samples_ref.at[:, pl.ds(g * span, span)], held.at[g], sems.at[g]
        )
        copy.start()
        return copy

    coef_copy = pltpu.make_async_copy(coef_hbm, coef_ref, sems.at[groups])
    coef_copy.start()
    loads = [load(0), load(1)]
    table_copy = pltpu.make_async_copy(table_hbm, table_ref, sems.at[groups + 1])
    table_copy.start()

    def filter_rows(g, i):
        rows = slice(i, i + ROWS)
        for n in range(0, fft, LANES):
            coefs = [coef_ref[p : p + 1, n : n + LANES] for p in range(taps)]

            def frame(f):
                where, k = f // GROUP, f % GROUP
                return held[where, rows, k * fft + n : k * fft + n + LANES].astype(jnp.float32)

            def share(f, known):
                total = None
                for p in range(taps):
                    if f - p in known:
                        term = coefs[p] * known[f - p]
                        total = term if total is None else total + term
                return total

            if g == 0:
                known = {f: frame(f) for f in range(GROUP)}
                for slot, f in enumerate(edge[:-AHEAD]):
                    partial_ref[slot, rows, n : n + LANES] = share(f, known)
                known = {f: frame(f) for f in range(frames + 1 - taps, frames)}
                for slot, f in enumerate(edge[-AHEAD:]):
                    partial_ref[slot + GROUP - AHEAD, rows, n : n + LANES] = share(f, known)
            else:
                known = {f: frame(f) for f in range(g * GROUP + 1 - taps, g * GROUP)}
                for slot in range(GROUP):
                    f = g * GROUP + slot
                    known[f] = frame(f)
                    filts[g % 2][slot, rows, n : n + LANES] = share(f, known).astype(jnp.bfloat16)

    results = []

    def send(g):
        copy = pltpu.make_async_copy(
            stage.at[g - 1], spectra_ref.at[:, pl.ds(g * GROUP, GROUP), :], out_sems.at[g - 1]
        )
        copy.start()
        results.append(copy)

    coef_copy.wait()
    loads[0].wait()
    order = [*range(1, groups), 0]
    pairs = GROUP // 2
    share_rows = inputs // pairs
    for at, g in enumerate(order):
        if g:
            loads[g].wait()
            if g + 1 < groups:
                loads.append(load(g + 1))
        if at == 1:
            table_copy.wait()
        for pair in range(pairs):
            if at >= 1:
                last = order[at - 1]
                transform_pair(filts[last % 2], 2 * pair, table_ref, spreads[last % 2])
            if at >= 2:
                before = order[at - 2]
                pack(spreads[before % 2], stage.at[before - 1], pair, pairs)
            for i in range(pair * share_rows, (pair + 1) * share_rows, ROWS):
                filter_rows(g, i)
        if at >= 2:
            send(order[at - 2])
    pack(spreads[order[-2] % 2], stage.at[order[-2] - 1], 0, 1)
    send(order[-2])
    for copy in results:
        copy.wait()


def edge_kernel(
    has_behind_ref, has_own_ref, behind_ref, ahead_ref, partial_ref, coef_ref, table_ref, _, spectra_ref,
    masked_ref, filt, spread, stage, sems, *, frames,
):
    taps, fft = coef_ref.shape
    inputs = behind_ref.shape[0]
    past = behind_ref.shape[1] // fft
    has_own = has_own_ref[0]
    edge = edge_frames(frames)
    masked_ref[...] = coef_ref[...] * has_behind_ref[0]

    for slot in range(0, GROUP, 2):
        for i in range(0, inputs, ROWS):
            rows = slice(i, i + ROWS)
            for n in range(0, fft, LANES):
                lanes = slice(n, n + LANES)
                samples = {}

                def frame(f):
                    if f not in samples:
                        ref, k = (behind_ref, f + past) if f < 0 else (ahead_ref, f - frames)
                        value = ref[rows, k * fft + n : k * fft + n + LANES]
                        samples[f] = value.astype(jnp.float32)
                    return samples[f]

                for s in (slot, slot + 1):
                    f = edge[s]
                    value = partial_ref[s, rows, lanes]
                    if f < frames:
                        for p in range(f + 1, taps):
                            value = value + masked_ref[p : p + 1, lanes] * frame(f - p)
                    else:
                        value = value * has_own
                        for p in range(f - frames + 1):
                            value = value + coef_ref[p : p + 1, lanes] * frame(f - p)
                    filt[s, rows, lanes] = value.astype(jnp.bfloat16)
        transform_pair(filt, slot, table_ref, spread)
    parts = sems.shape[0]
    copies = []
    for part in range(parts):
        pack(spread, stage, part, parts)
        rows = pl.ds(part * (fft // parts), fft // parts)
        copy = pltpu.make_async_copy(
            stage.at[rows], spectra_ref.at[rows, pl.ds(0, GROUP), :], sems.at[part]
        )
        copy.start()
        copies.append(copy)
    for copy in copies:
        copy.wait()


def correlate_kernel(recv_ref, out_ref, held, turned, swapped, stage, sems):
    tm_count, input_count, items, _, frames, inputs = recv_ref.shape
    half = tm_count * frames
    width = input_count * inputs
    scale = 1.0 / half
    copies = []

    def give(c, part, i, j, value):
        rows, cols = pl.ds(i, BLOCK), pl.ds(j, BLOCK)
        stage[c, part, rows, cols] = value.astype(jnp.bfloat16)
        copy = pltpu.make_async_copy(
            stage.at[c, part, rows, cols], out_ref.at[c, part, rows, cols], sems.at[len(copies)]
        )
        copy.start()
        copies.append(copy)

    for c in range(items):
        for r in range(2):
            for a in range(tm_count):
                for b in range(input_count):
                    rows = slice(r * half + a * frames, r * half + (a + 1) * frames)
                    cols = slice(b * inputs, (b + 1) * inputs)
                    held[c, rows, cols] = recv_ref[a, b, c, r]
        turned[c] = held[c].T
        swapped[c, :half] = -held[c, half:]
        swapped[c, half:] = held[c, :half]
        for i in range(0, width, BLOCK):
            for j in range(i, width, BLOCK):
                left = turned[c, i : i + BLOCK]
                real = scale * jnp.dot(
                    left, held[c, :, j : j + BLOCK], preferred_element_type=jnp.float32
                )
                if j > i:
                    imag = scale * jnp.dot(
                        left, swapped[c, :, j : j + BLOCK], preferred_element_type=jnp.float32
                    )
                else:
                    cross = scale * jnp.dot(
                        turned[c, i : i + BLOCK, half:],
                        held[c, :half, j : j + BLOCK],
                        preferred_element_type=jnp.float32,
                    )
                    imag = cross - cross.T
                give(c, 0, i, j, real)
                give(c, 1, i, j, imag)
                if j > i:
                    give(c, 0, j, i, real.T)
                    give(c, 1, j, i, -imag.T)
    for copy in copies:
        copy.wait()


def local(samples, coefficients):
    inputs, sample_count = samples.shape
    taps, fft = coefficients.shape
    frames = sample_count // fft
    tm_count = lax.axis_size("tm")
    input_count = lax.axis_size("input")
    devices = tm_count * input_count
    groups = frames // GROUP
    past = (taps - 1 - AHEAD) * fft
    ahead = AHEAD * fft
    table = jnp.asarray(dft_table(fft))
    vmem = pl.BlockSpec(memory_space=pltpu.VMEM)
    smem = pl.BlockSpec(memory_space=pltpu.SMEM)
    hbm = pl.BlockSpec(memory_space=pltpu.HBM)

    ring = [(i, (i + 1) % tm_count) for i in range(tm_count)]
    own_tm = lax.axis_index("tm")
    has_behind = jnp.where(own_tm > 0, 1.0, 0.0).astype(jnp.float32).reshape(1)
    has_own = jnp.where(own_tm < tm_count - 1, 1.0, 0.0).astype(jnp.float32).reshape(1)
    spectra_type = pltpu.HBM((fft, frames, inputs), jnp.bfloat16)
    in_hbm = lambda array: pltpu.with_memory_space_constraint(array, pltpu.HBM)
    filt = pltpu.VMEM((GROUP, inputs, fft), jnp.bfloat16)
    spread = pltpu.VMEM((fft * GROUP, inputs), jnp.float32)
    last, first = pl.pallas_call(
        tails_kernel,
        in_specs=[hbm],
        out_specs=[vmem, vmem],
        out_shape=[
            pltpu.VMEM((inputs, past), jnp.bfloat16),
            pltpu.VMEM((inputs, ahead), jnp.bfloat16),
        ],
        scratch_shapes=[
            pltpu.VMEM((inputs, past), jnp.int32),
            pltpu.VMEM((inputs, ahead), jnp.int32),
            pltpu.SemaphoreType.DMA((2,)),
        ],
        compiler_params=pltpu.CompilerParams(vmem_limit_bytes=8 << 20),
        name="tails",
    )(in_hbm(samples))
    from_behind = lax.ppermute(last, "tm", ring)
    from_ahead = lax.ppermute(first, "tm", [(b, a) for a, b in ring])

    spectra, partial = pl.pallas_call(
        own_kernel,
        in_specs=[hbm, hbm, hbm],
        out_specs=[hbm, vmem],
        out_shape=[spectra_type, pltpu.VMEM((GROUP, inputs, fft), jnp.float32)],
        scratch_shapes=[
            pltpu.VMEM((taps, fft), jnp.float32),
            pltpu.VMEM((fft, fft), jnp.bfloat16),
            pltpu.VMEM((groups, inputs, GROUP * fft), jnp.int32),
            [filt, filt],
            [spread, spread],
            pltpu.VMEM((groups - 1, fft, GROUP, inputs), jnp.bfloat16),
            pltpu.SemaphoreType.DMA((groups + 2,)),
            pltpu.SemaphoreType.DMA((groups - 1,)),
        ],
        compiler_params=pltpu.CompilerParams(vmem_limit_bytes=24 << 20),
        name="own_frames",
    )(in_hbm(samples), in_hbm(coefficients), in_hbm(table))
    spectra = pl.pallas_call(
        functools.partial(edge_kernel, frames=frames),
        in_specs=[smem] * 2 + [vmem] * 5 + [hbm],
        out_specs=hbm,
        out_shape=spectra_type,
        scratch_shapes=[
            pltpu.VMEM((taps, fft), jnp.float32),
            filt,
            spread,
            pltpu.VMEM((fft, GROUP, inputs), jnp.bfloat16),
            pltpu.SemaphoreType.DMA((4,)),
        ],
        input_output_aliases={7: 0},
        compiler_params=pltpu.CompilerParams(vmem_limit_bytes=16 << 20),
        name="edge_frames",
    )(has_behind, has_own, from_behind, from_ahead, partial, coefficients, table, spectra)

    items = fft // (2 * devices)
    outgoing = spectra.reshape(devices, 2 * items, frames, inputs)
    received = lax.all_to_all(outgoing, ("tm", "input"), 0, 0, tiled=True)
    received = received.reshape(tm_count, input_count, items, 2, frames, inputs)
    depth = 2 * tm_count * frames
    width = input_count * inputs
    blocks = (width // BLOCK) ** 2
    return pl.pallas_call(
        correlate_kernel,
        in_specs=[vmem],
        out_specs=hbm,
        out_shape=jax.ShapeDtypeStruct((items, 2, width, width), jnp.bfloat16),
        scratch_shapes=[
            pltpu.VMEM((items, depth, width), jnp.bfloat16),
            pltpu.VMEM((items, width, depth), jnp.bfloat16),
            pltpu.VMEM((items, depth, width), jnp.bfloat16),
            pltpu.VMEM((items, 2, width, width), jnp.bfloat16),
            pltpu.SemaphoreType.DMA((2 * items * blocks,)),
        ],
        compiler_params=pltpu.CompilerParams(vmem_limit_bytes=36 << 20),
        name="correlate",
    )(received)


def solution(mesh):
    in_specs = (P("input", "tm"), P())
    out_specs = P(("tm", "input"), None, None, None)
    return jax.shard_map(local, mesh=mesh, in_specs=in_specs, out_specs=out_specs, check_vma=False)
```

time: 92.4 us -> 87.5 us (0.947)
  Pallas kernels: 25.9 us -> 20.7 us
    pallas_call x1, Pallas kernels: 13.6 us -> 10.2 us  [local(): pl.pallas_call(own_kernel, in_specs=[hbm, hbm, hbm], out_specs=[hbm, vmem...]
    pallas_call x1, Pallas kernels: 2.83 us -> 1.91 us  [local(): pl.pallas_call(functools.partial(edge_kernel, frames=frames), in_specs=[s...]
  transfers between devices with their start and end apart: 2 -> 2, of which waited for: 0 -> 0; matrix products, arithmetic and copies ran while one was open for 0% -> 0% of each run, Pallas kernels for 15% -> 12%
where the time goes in v5:
time: 87.5 us; the launch traced here: 87.2 us
  blocking collectives  60.8 us (69%)
  Pallas kernels  20.7 us (24%)
  starting transfers between devices  5.42 us (6%)
    all_to_all x1, blocking collectives, local(): received = lax.all_to_all(outgoing, ('tm', 'input'), 0, 0, tiled=True)  60.8 us
    pallas_call x1, Pallas kernels, local(): pl.pallas_call(own_kernel, in_specs=[hbm, hbm, hbm], out_specs=[hbm, vmem...  10.2 us
    pallas_call x1, Pallas kernels, local(): pl.pallas_call(correlate_kernel, in_specs=[vmem], out_specs=hbm, out_shap...  7.15 us
    ppermute x1, starting transfers between devices, local(): from_ahead = lax.ppermute(first, 'tm', [(b, a) for a, b in ring])  5.35 us
    pallas_call x1, Pallas kernels, local(): pl.pallas_call(functools.partial(edge_kernel, frames=frames), in_specs=[s...  1.91 us
  transfers between devices with their start and end apart: 2, of which 0 were waited for; matrix products, arithmetic and copies ran while one was open for 0% of the time, Pallas kernels for 12%

profile of v5, /device:TPU:0, one launch (start us, length us, event | category | flops | bytes accessed | tf_op | source)
XLA Modules:
  0.0 87.2 jit_solution(507908286368978991)
XLA Ops:
  0.0 1.5 %tails.1 = (bf16[128,2048]{1,0:T(8,128)(2,1)S(1)}, bf16[128,1536]{1,0:T(8,128)(2,1)S(1)}) custom-call(s32[128,16384]{1,0:T(8,128)} %samples_ref.3), custom_call_target="tpu_custom_call" | custom-call | tf_op jit(solution)/shard_map/tails/pallas_call | solution.py:283
  1.5 0.1 collective-permute-start
  1.6 5.3 %collective-permute-start.1 = (bf16[128,1536]{1,0:T(8,128)(2,1)S(1)}, bf16[128,1536]{1,0:T(8,128)(2,1)S(1)}, u32[]{:S(2)}, u32[]{:S(2)}) collective-permute-start(bf16[128,1536]{1,0:T(8,128)(2,1)S(1)} %get-tuple-element.10), channel_id=1, source_target_pairs={{8,0},{16,8},{24,16},{32,24},{40,32},{48,40},{56,48},{64,56},{72,6... | collective-permute-start | bytes 1179656 | tf_op jit(solution)/shard_map/ppermute | solution.py:300
  6.9 0.0 copy-start
  6.9 0.0 copy-start.1
  6.9 10.2 %own_frames.1 = (bf16[512,32,128]{2,1,0:T(8,128)(2,1)}, f32[8,128,512]{2,1,0:T(8,128)S(1)}) custom-call(s32[128,16384]{1,0:T(8,128)} %samples_ref.3, f32[8,512]{1,0:T(8,128)} %coef_ref.1, bf16[512,512]{1,0:T(8,128)(2,1)} %constant.16.clone.table_hbm.table_ref), custom_call_target="tpu_custom_call" | custom-call | tf_op jit(solution)/shard_map/own_frames/pallas_call | solution.py:302
  17.1 0.0 collective-permute-done.1.ahead_ref
  17.1 0.0 collective-permute-done.behind_ref
  17.1 0.0 copy-done
  17.2 0.0 copy-done.1
  17.2 1.9 %edge_frames.1 = bf16[512,32,128]{2,1,0:T(8,128)(2,1)} custom-call(f32[1]{0:T(128)} %bitcast.has_behind_ref, f32[1]{0:T(128)} %bitcast.1.has_own_ref, bf16[128,2048]{1,0:T(8,128)(2,1)S(1)} %collective-permute-done.behind_ref, bf16[128,1536]{1,0:T(8,128)(2,1)S(1)} %collective-permute-done.1.ahead_ref, ...), custom_call_target="tpu_custom_call", output_to_operand_aliasing={{}: (7, {})} | custom-call | tf_op jit(solution)/shard_map/edge_frames/pallas_call | solution.py:320
  19.1 60.8 %all_to_all.5 = bf16[128,4,32,128]{3,2,1,0:T(8,128)(2,1)S(1)} all-to-all(bf16[128,4,32,128]{3,2,1,0:T(8,128)(2,1)} %bitcast.5), channel_id=1, replica_groups=mesh['tm'=16,'input'=8] {'tm','input'}, dimensions={0} | all-to-all | bytes 8388608 | tf_op jit(solution)/shard_map/all_to_all | solution.py:339
  79.9 7.2 %correlate.1 = bf16[2,2,1024,1024]{3,2,1,0:T(8,128)(2,1)} custom-call(bf16[16,8,2,2,32,128]{5,4,3,2,1,0:T(8,128)(2,1)S(1)} %bitcast.4), custom_call_target="tpu_custom_call" | custom-call | tf_op jit(solution)/shard_map/correlate/pallas_call | solution.py:344
Async XLA Ops:
  1.5 15.6 %collective-permute-start = (bf16[128,2048]{1,0:T(8,128)(2,1)S(1)}, bf16[128,2048]{1,0:T(8,128)(2,1)S(1)}, u32[]{:S(2)}, u32[]{:S(2)}) collective-permute-start(bf16[128,2048]{1,0:T(8,128)(2,1)S(1)} %get-tuple-element.9), channel_id=1, source_target_pairs={{0,8},{8,16},{16,24},{24,32},{32,40},{40,48},{48,56},{56,64},{64,7... | collective-permute-start | bytes 1572872 | tf_op jit(solution)/shard_map/ppermute | solution.py:299
  1.6 15.5 %collective-permute-start.1 = (bf16[128,1536]{1,0:T(8,128)(2,1)S(1)}, bf16[128,1536]{1,0:T(8,128)(2,1)S(1)}, u32[]{:S(2)}, u32[]{:S(2)}) collective-permute-start(bf16[128,1536]{1,0:T(8,128)(2,1)S(1)} %get-tuple-element.10), channel_id=1, source_target_pairs={{8,0},{16,8},{24,16},{32,24},{40,32},{48,40},{56,48},{64,56},{72,6... | collective-permute-start | bytes 1179656 | tf_op jit(solution)/shard_map/ppermute | solution.py:300
  6.9 10.2 %copy-start = (bf16[512,512]{1,0:T(8,128)(2,1)S(1)}, bf16[512,512]{1,0:T(8,128)(2,1)}, u32[]{:S(2)}) copy-start(bf16[512,512]{1,0:T(8,128)(2,1)} %constant.16.clone.table_hbm.table_ref) | copy-start | bytes 1572868
  6.9 10.2 %copy-start.1 = (f32[8,512]{1,0:T(8,128)S(1)}, f32[8,512]{1,0:T(8,128)}, u32[]{:S(2)}) copy-start(f32[8,512]{1,0:T(8,128)} %coef_ref.1) | copy-start | bytes 49156

commit v6 on v5

--- a/solution.py
+++ b/solution.py
@@ -68,22 +68,35 @@
     coef_ref, table_ref, held, filts, spreads, stage, sems, out_sems,
 ):
     taps, fft = coef_ref.shape
-    groups, inputs, span = held.shape
-    frames = groups * GROUP
+    inputs, count = held.shape
+    frames = count // fft
+    groups = frames // GROUP
+    span = GROUP * fft
     edge = edge_frames(frames)
-
-    def load(g):
-        copy = pltpu.make_async_copy(
-            samples_ref.at[:, pl.ds(g * span, span)], held.at[g], sems.at[g]
+    pairs = GROUP // 2
+    chunk = inputs // pairs
+
+    boxes = [(slice(k * chunk, (k + 1) * chunk), slice(0, 2 * span)) for k in range(pairs)]
+    boxes += [(slice(0, inputs), slice(g * span, (g + 1) * span)) for g in range(2, groups)]
+    loads = [
+        pltpu.make_async_copy(
+            samples_ref.at[pl.ds(r.start, r.stop - r.start), pl.ds(c.start, c.stop - c.start)],
+            held.at[pl.ds(r.start, r.stop - r.start), pl.ds(c.start, c.stop - c.start)],
+            sems.at[k],
         )
-        copy.start()
-        return copy
-
-    coef_copy = pltpu.make_async_copy(coef_hbm, coef_ref, sems.at[groups])
+        for k, (r, c) in enumerate(boxes)
+    ]
+    coef_copy = pltpu.make_async_copy(coef_hbm, coef_ref, sems.at[len(loads)])
+    table_copy = pltpu.make_async_copy(table_hbm, table_ref, sems.at[len(loads) + 1])
     coef_copy.start()
-    loads = [load(0), load(1)]
-    table_copy = pltpu.make_async_copy(table_hbm, table_ref, sems.at[groups + 1])
+    loads[0].start()
+    loads[1].start()
     table_copy.start()
+
+    def arrive(k):
+        loads[k].wait()
+        if k + 2 < len(loads):
+            loads[k + 2].start()
 
     def filter_rows(g, i):
         rows = slice(i, i + ROWS)
@@ -91,8 +104,7 @@
             coefs = [coef_ref[p : p + 1, n : n + LANES] for p in range(taps)]
 
             def frame(f):
-                where, k = f // GROUP, f % GROUP
-                return held[where, rows, k * fft + n : k * fft + n + LANES].astype(jnp.float32)
+                return held[rows, f * fft + n : f * fft + n + LANES].astype(jnp.float32)
 
             def share(f, known):
                 total = None
@@ -118,38 +130,44 @@
 
     results = []
 
-    def send(g):
+    def send(g, part=0, parts=1):
+        rows = pl.ds(part * (fft // parts), fft // parts)
         copy = pltpu.make_async_copy(
-            stage.at[g - 1], spectra_ref.at[:, pl.ds(g * GROUP, GROUP), :], out_sems.at[g - 1]
+            stage.at[g - 1, rows],
+            spectra_ref.at[rows, pl.ds(g * GROUP, GROUP), :],
+            out_sems.at[len(results)],
         )
         copy.start()
         results.append(copy)
 
     coef_copy.wait()
-    loads[0].wait()
-    order = [*range(1, groups), 0]
-    pairs = GROUP // 2
-    share_rows = inputs // pairs
-    for at, g in enumerate(order):
-        if g:
-            loads[g].wait()
-            if g + 1 < groups:
-                loads.append(load(g + 1))
-        if at == 1:
+    for g in range(1, groups):
+        if g == 2:
             table_copy.wait()
+        if g >= 2:
+            arrive(pairs + g - 2)
         for pair in range(pairs):
-            if at >= 1:
-                last = order[at - 1]
-                transform_pair(filts[last % 2], 2 * pair, table_ref, spreads[last % 2])
-            if at >= 2:
-                before = order[at - 2]
-                pack(spreads[before % 2], stage.at[before - 1], pair, pairs)
-            for i in range(pair * share_rows, (pair + 1) * share_rows, ROWS):
+            if g >= 2:
+                transform_pair(filts[(g - 1) % 2], 2 * pair, table_ref, spreads[(g - 1) % 2])
+            if g >= 3:
+                pack(spreads[g % 2], stage.at[g - 3], pair, pairs)
+            if g == 1:
+                arrive(pair)
+            for i in range(pair * chunk, (pair + 1) * chunk, ROWS):
                 filter_rows(g, i)
-        if at >= 2:
-            send(order[at - 2])
-    pack(spreads[order[-2] % 2], stage.at[order[-2] - 1], 0, 1)
-    send(order[-2])
+        if g >= 3:
+            send(g - 2)
+    last = groups - 1
+    step = chunk // 2
+    for pair in range(pairs):
+        transform_pair(filts[last % 2], 2 * pair, table_ref, spreads[last % 2])
+        pack(spreads[(last - 1) % 2], stage.at[last - 2], pair, pairs)
+        filter_rows(0, pair * step)
+    send(last - 1)
+    for pair in range(pairs):
+        pack(spreads[last % 2], stage.at[last - 1], pair, pairs)
+        send(last, pair, pairs)
+        filter_rows(0, (pairs + pair) * step)
     for copy in results:
         copy.wait()
 
@@ -307,12 +325,12 @@
         scratch_shapes=[
             pltpu.VMEM((taps, fft), jnp.float32),
             pltpu.VMEM((fft, fft), jnp.bfloat16),
-            pltpu.VMEM((groups, inputs, GROUP * fft), jnp.int32),
+            pltpu.VMEM((inputs, sample_count), jnp.int32),
             [filt, filt],
             [spread, spread],
             pltpu.VMEM((groups - 1, fft, GROUP, inputs), jnp.bfloat16),
-            pltpu.SemaphoreType.DMA((groups + 2,)),
-            pltpu.SemaphoreType.DMA((groups - 1,)),
+            pltpu.SemaphoreType.DMA((GROUP // 2 + groups,)),
+            pltpu.SemaphoreType.DMA((groups + GROUP // 2,)),
         ],
         compiler_params=pltpu.CompilerParams(vmem_limit_bytes=24 << 20),
         name="own_frames",

time: 87.5 us -> 87.5 us (level)
  no operation moved by 1% of the time
where the time goes in v6:
time: 87.5 us; the launch traced here: 87.2 us
  blocking collectives  60.8 us (69%)
  Pallas kernels  20.8 us (24%)
  starting transfers between devices  5.42 us (6%)
    all_to_all x1, blocking collectives, local(): received = lax.all_to_all(outgoing, ('tm', 'input'), 0, 0, tiled=True)  60.8 us
    pallas_call x1, Pallas kernels, local(): pl.pallas_call(own_kernel, in_specs=[hbm, hbm, hbm], out_specs=[hbm, vmem...  10.2 us
    pallas_call x1, Pallas kernels, local(): pl.pallas_call(correlate_kernel, in_specs=[vmem], out_specs=hbm, out_shap...  7.15 us
    ppermute x1, starting transfers between devices, local(): from_ahead = lax.ppermute(first, 'tm', [(b, a) for a, b in ring])  5.35 us
    pallas_call x1, Pallas kernels, local(): pl.pallas_call(functools.partial(edge_kernel, frames=frames), in_specs=[s...  1.91 us
  transfers between devices with their start and end apart: 2, of which 0 were waited for; matrix products, arithmetic and copies ran while one was open for 0% of the time, Pallas kernels for 12%

profile of v6, /device:TPU:0, one launch (start us, length us, event | category | flops | bytes accessed | tf_op | source)
XLA Modules:
  0.0 87.2 jit_solution(149720271263555093)
XLA Ops:
  0.0 1.5 %tails.1 = (bf16[128,2048]{1,0:T(8,128)(2,1)S(1)}, bf16[128,1536]{1,0:T(8,128)(2,1)S(1)}) custom-call(s32[128,16384]{1,0:T(8,128)} %samples_ref.3), custom_call_target="tpu_custom_call" | custom-call | tf_op jit(solution)/shard_map/tails/pallas_call | solution.py:301
  1.5 0.1 collective-permute-start
  1.6 5.3 %collective-permute-start.1 = (bf16[128,1536]{1,0:T(8,128)(2,1)S(1)}, bf16[128,1536]{1,0:T(8,128)(2,1)S(1)}, u32[]{:S(2)}, u32[]{:S(2)}) collective-permute-start(bf16[128,1536]{1,0:T(8,128)(2,1)S(1)} %get-tuple-element.10), channel_id=1, source_target_pairs={{8,0},{16,8},{24,16},{32,24},{40,32},{48,40},{56,48},{64,56},{72,6... | collective-permute-start | bytes 1179656 | tf_op jit(solution)/shard_map/ppermute | solution.py:318
  6.9 0.0 copy-start
  6.9 0.0 copy-start.1
  6.9 10.2 %own_frames.1 = (bf16[512,32,128]{2,1,0:T(8,128)(2,1)}, f32[8,128,512]{2,1,0:T(8,128)S(1)}) custom-call(s32[128,16384]{1,0:T(8,128)} %samples_ref.3, f32[8,512]{1,0:T(8,128)} %coef_ref.1, bf16[512,512]{1,0:T(8,128)(2,1)} %constant.16.clone.table_hbm.table_ref), custom_call_target="tpu_custom_call" | custom-call | tf_op jit(solution)/shard_map/own_frames/pallas_call | solution.py:320
  17.2 0.0 collective-permute-done.1.ahead_ref
  17.2 0.0 collective-permute-done.behind_ref
  17.2 0.0 copy-done
  17.2 0.0 copy-done.1
  17.2 1.9 %edge_frames.1 = bf16[512,32,128]{2,1,0:T(8,128)(2,1)} custom-call(f32[1]{0:T(128)} %bitcast.has_behind_ref, f32[1]{0:T(128)} %bitcast.1.has_own_ref, bf16[128,2048]{1,0:T(8,128)(2,1)S(1)} %collective-permute-done.behind_ref, bf16[128,1536]{1,0:T(8,128)(2,1)S(1)} %collective-permute-done.1.ahead_ref, ...), custom_call_target="tpu_custom_call", output_to_operand_aliasing={{}: (7, {})} | custom-call | tf_op jit(solution)/shard_map/edge_frames/pallas_call | solution.py:338
  19.1 60.8 %all_to_all.5 = bf16[128,4,32,128]{3,2,1,0:T(8,128)(2,1)S(1)} all-to-all(bf16[128,4,32,128]{3,2,1,0:T(8,128)(2,1)} %bitcast.5), channel_id=1, replica_groups=mesh['tm'=16,'input'=8] {'tm','input'}, dimensions={0} | all-to-all | bytes 8388608 | tf_op jit(solution)/shard_map/all_to_all | solution.py:357
  79.9 7.1 %correlate.1 = bf16[2,2,1024,1024]{3,2,1,0:T(8,128)(2,1)} custom-call(bf16[16,8,2,2,32,128]{5,4,3,2,1,0:T(8,128)(2,1)S(1)} %bitcast.4), custom_call_target="tpu_custom_call" | custom-call | tf_op jit(solution)/shard_map/correlate/pallas_call | solution.py:362
Async XLA Ops:
  1.5 15.7 %collective-permute-start = (bf16[128,2048]{1,0:T(8,128)(2,1)S(1)}, bf16[128,2048]{1,0:T(8,128)(2,1)S(1)}, u32[]{:S(2)}, u32[]{:S(2)}) collective-permute-start(bf16[128,2048]{1,0:T(8,128)(2,1)S(1)} %get-tuple-element.9), channel_id=1, source_target_pairs={{0,8},{8,16},{16,24},{24,32},{32,40},{40,48},{48,56},{56,64},{64,7... | collective-permute-start | bytes 1572872 | tf_op jit(solution)/shard_map/ppermute | solution.py:317
  1.6 15.6 %collective-permute-start.1 = (bf16[128,1536]{1,0:T(8,128)(2,1)S(1)}, bf16[128,1536]{1,0:T(8,128)(2,1)S(1)}, u32[]{:S(2)}, u32[]{:S(2)}) collective-permute-start(bf16[128,1536]{1,0:T(8,128)(2,1)S(1)} %get-tuple-element.10), channel_id=1, source_target_pairs={{8,0},{16,8},{24,16},{32,24},{40,32},{48,40},{56,48},{64,56},{72,6... | collective-permute-start | bytes 1179656 | tf_op jit(solution)/shard_map/ppermute | solution.py:318
  6.9 10.3 %copy-start = (bf16[512,512]{1,0:T(8,128)(2,1)S(1)}, bf16[512,512]{1,0:T(8,128)(2,1)}, u32[]{:S(2)}) copy-start(bf16[512,512]{1,0:T(8,128)(2,1)} %constant.16.clone.table_hbm.table_ref) | copy-start | bytes 1572868
  6.9 10.3 %copy-start.1 = (f32[8,512]{1,0:T(8,128)S(1)}, f32[8,512]{1,0:T(8,128)}, u32[]{:S(2)}) copy-start(f32[8,512]{1,0:T(8,128)} %coef_ref.1) | copy-start | bytes 49156

commit v7 on v6

--- a/solution.py
+++ b/solution.py
@@ -54,18 +54,17 @@
     spread[pl.ds(f + 1, fft, stride=frames), :] = spectra[:, inputs:]
 
 
-def pack(spread, stage, part, parts):
-    rows, frames, inputs = stage.shape
+def pack(spread, spectra_ref, group, part, parts):
+    rows, _, inputs = spectra_ref.shape
     count = rows // parts
-    block = spread[part * count * frames : (part + 1) * count * frames, :]
-    stage[part * count : (part + 1) * count] = block.reshape(count, frames, inputs).astype(
-        jnp.bfloat16
-    )
+    block = spread[part * count * GROUP : (part + 1) * count * GROUP, :]
+    where = (slice(part * count, (part + 1) * count), slice(group * GROUP, (group + 1) * GROUP))
+    spectra_ref[where] = block.reshape(count, GROUP, inputs).astype(jnp.bfloat16)
 
 
 def own_kernel(
     samples_ref, coef_hbm, table_hbm, spectra_ref, partial_ref,
-    coef_ref, table_ref, held, filts, spreads, stage, sems, out_sems,
+    coef_ref, table_ref, held, filts, spreads, sems,
 ):
     taps, fft = coef_ref.shape
     inputs, count = held.shape
@@ -89,14 +88,14 @@
     coef_copy = pltpu.make_async_copy(coef_hbm, coef_ref, sems.at[len(loads)])
     table_copy = pltpu.make_async_copy(table_hbm, table_ref, sems.at[len(loads) + 1])
     coef_copy.start()
-    loads[0].start()
-    loads[1].start()
+    for load in loads[:3]:
+        load.start()
     table_copy.start()
 
     def arrive(k):
         loads[k].wait()
-        if k + 2 < len(loads):
-            loads[k + 2].start()
+        if k + 3 < len(loads):
+            loads[k + 3].start()
 
     def filter_rows(g, i):
         rows = slice(i, i + ROWS)
@@ -128,18 +127,6 @@
                     known[f] = frame(f)
                     filts[g % 2][slot, rows, n : n + LANES] = share(f, known).astype(jnp.bfloat16)
 
-    results = []
-
-    def send(g, part=0, parts=1):
-        rows = pl.ds(part * (fft // parts), fft // parts)
-        copy = pltpu.make_async_copy(
-            stage.at[g - 1, rows],
-            spectra_ref.at[rows, pl.ds(g * GROUP, GROUP), :],
-            out_sems.at[len(results)],
-        )
-        copy.start()
-        results.append(copy)
-
     coef_copy.wait()
     for g in range(1, groups):
         if g == 2:
@@ -150,31 +137,23 @@
             if g >= 2:
                 transform_pair(filts[(g - 1) % 2], 2 * pair, table_ref, spreads[(g - 1) % 2])
             if g >= 3:
-                pack(spreads[g % 2], stage.at[g - 3], pair, pairs)
+                pack(spreads[g % 2], spectra_ref, g - 2, pair, pairs)
             if g == 1:
                 arrive(pair)
             for i in range(pair * chunk, (pair + 1) * chunk, ROWS):
                 filter_rows(g, i)
-        if g >= 3:
-            send(g - 2)
     last = groups - 1
-    step = chunk // 2
     for pair in range(pairs):
         transform_pair(filts[last % 2], 2 * pair, table_ref, spreads[last % 2])
-        pack(spreads[(last - 1) % 2], stage.at[last - 2], pair, pairs)
-        filter_rows(0, pair * step)
-    send(last - 1)
-    for pair in range(pairs):
-        pack(spreads[last % 2], stage.at[last - 1], pair, pairs)
-        send(last, pair, pairs)
-        filter_rows(0, (pairs + pair) * step)
-    for copy in results:
-        copy.wait()
+        pack(spreads[(last - 1) % 2], spectra_ref, last - 1, pair, pairs)
+        filter_rows(0, pair * 2 * ROWS)
+        filter_rows(0, pair * 2 * ROWS + ROWS)
+    pack(spreads[last % 2], spectra_ref, last, 0, 1)
 
 
 def edge_kernel(
     has_behind_ref, has_own_ref, behind_ref, ahead_ref, partial_ref, coef_ref, table_ref, _, spectra_ref,
-    masked_ref, filt, spread, stage, sems, *, frames,
+    masked_ref, filt, spread, *, frames,
 ):
     taps, fft = coef_ref.shape
     inputs = behind_ref.shape[0]
@@ -209,18 +188,7 @@
                             value = value + coef_ref[p : p + 1, lanes] * frame(f - p)
                     filt[s, rows, lanes] = value.astype(jnp.bfloat16)
         transform_pair(filt, slot, table_ref, spread)
-    parts = sems.shape[0]
-    copies = []
-    for part in range(parts):
-        pack(spread, stage, part, parts)
-        rows = pl.ds(part * (fft // parts), fft // parts)
-        copy = pltpu.make_async_copy(
-            stage.at[rows], spectra_ref.at[rows, pl.ds(0, GROUP), :], sems.at[part]
-        )
-        copy.start()
-        copies.append(copy)
-    for copy in copies:
-        copy.wait()
+    pack(spread, spectra_ref, 0, 0, 1)
 
 
 def correlate_kernel(recv_ref, out_ref, held, turned, swapped, stage, sems):
@@ -294,7 +262,7 @@
     own_tm = lax.axis_index("tm")
     has_behind = jnp.where(own_tm > 0, 1.0, 0.0).astype(jnp.float32).reshape(1)
     has_own = jnp.where(own_tm < tm_count - 1, 1.0, 0.0).astype(jnp.float32).reshape(1)
-    spectra_type = pltpu.HBM((fft, frames, inputs), jnp.bfloat16)
+    spectra_type = pltpu.VMEM((fft, frames, inputs), jnp.bfloat16)
     in_hbm = lambda array: pltpu.with_memory_space_constraint(array, pltpu.HBM)
     filt = pltpu.VMEM((GROUP, inputs, fft), jnp.bfloat16)
     spread = pltpu.VMEM((fft * GROUP, inputs), jnp.float32)
@@ -320,7 +288,7 @@
     spectra, partial = pl.pallas_call(
         own_kernel,
         in_specs=[hbm, hbm, hbm],
-        out_specs=[hbm, vmem],
+        out_specs=[vmem, vmem],
         out_shape=[spectra_type, pltpu.VMEM((GROUP, inputs, fft), jnp.float32)],
         scratch_shapes=[
             pltpu.VMEM((taps, fft), jnp.float32),
@@ -328,24 +296,20 @@
             pltpu.VMEM((inputs, sample_count), jnp.int32),
             [filt, filt],
             [spread, spread],
-            pltpu.VMEM((groups - 1, fft, GROUP, inputs), jnp.bfloat16),
             pltpu.SemaphoreType.DMA((GROUP // 2 + groups,)),
-            pltpu.SemaphoreType.DMA((groups + GROUP // 2,)),
         ],
         compiler_params=pltpu.CompilerParams(vmem_limit_bytes=24 << 20),
         name="own_frames",
     )(in_hbm(samples), in_hbm(coefficients), in_hbm(table))
     spectra = pl.pallas_call(
         functools.partial(edge_kernel, frames=frames),
-        in_specs=[smem] * 2 + [vmem] * 5 + [hbm],
-        out_specs=hbm,
+        in_specs=[smem] * 2 + [vmem] * 6,
+        out_specs=vmem,
         out_shape=spectra_type,
         scratch_shapes=[
             pltpu.VMEM((taps, fft), jnp.float32),
             filt,
             spread,
-            pltpu.VMEM((fft, GROUP, inputs), jnp.bfloat16),
-            pltpu.SemaphoreType.DMA((4,)),
         ],
         input_output_aliases={7: 0},
         compiler_params=pltpu.CompilerParams(vmem_limit_bytes=16 << 20),

time: 87.5 us -> 84.7 us (0.968)
  Pallas kernels: 20.8 us -> 18.4 us
    pallas_call x1, Pallas kernels: 10.2 us -> 8.59 us  [local(): pl.pallas_call(own_kernel, in_specs=[hbm, hbm, hbm], out_specs=[vmem, vme...]
  transfers between devices with their start and end apart: 2 -> 2, of which waited for: 0 -> 0; matrix products, arithmetic and copies ran while one was open for 0% -> 0% of each run, Pallas kernels for 12% -> 10%
where the time goes in v7:
time: 84.7 us; the launch traced here: 84.6 us
  blocking collectives  60.6 us (72%)
  Pallas kernels  18.4 us (22%)
  starting transfers between devices  5.42 us (6%)
    all_to_all x1, blocking collectives, local(): received = lax.all_to_all(outgoing, ('tm', 'input'), 0, 0, tiled=True)  60.6 us
    pallas_call x1, Pallas kernels, local(): pl.pallas_call(own_kernel, in_specs=[hbm, hbm, hbm], out_specs=[vmem, vme...  8.59 us
    pallas_call x1, Pallas kernels, local(): pl.pallas_call(correlate_kernel, in_specs=[vmem], out_specs=hbm, out_shap...  7.15 us
    ppermute x1, starting transfers between devices, local(): from_ahead = lax.ppermute(first, 'tm', [(b, a) for a, b in ring])  5.35 us
  transfers between devices with their start and end apart: 2, of which 0 were waited for; matrix products, arithmetic and copies ran while one was open for 0% of the time, Pallas kernels for 10%

profile of v7, /device:TPU:0, one launch (start us, length us, event | category | flops | bytes accessed | tf_op | source)
XLA Modules:
  0.0 84.6 jit_solution(5368872924468500097)
XLA Ops:
  0.0 1.5 %tails.1 = (bf16[128,2048]{1,0:T(8,128)(2,1)S(1)}, bf16[128,1536]{1,0:T(8,128)(2,1)S(1)}) custom-call(s32[128,16384]{1,0:T(8,128)} %samples_ref.3), custom_call_target="tpu_custom_call" | custom-call | tf_op jit(solution)/shard_map/tails/pallas_call | solution.py:269
  1.5 0.1 collective-permute-start
  1.6 5.3 %collective-permute-start.1 = (bf16[128,1536]{1,0:T(8,128)(2,1)S(1)}, bf16[128,1536]{1,0:T(8,128)(2,1)S(1)}, u32[]{:S(2)}, u32[]{:S(2)}) collective-permute-start(bf16[128,1536]{1,0:T(8,128)(2,1)S(1)} %get-tuple-element.10), channel_id=1, source_target_pairs={{8,0},{16,8},{24,16},{32,24},{40,32},{48,40},{56,48},{64,56},{72,6... | collective-permute-start | bytes 1179656 | tf_op jit(solution)/shard_map/ppermute | solution.py:286
  6.9 0.0 copy-start
  6.9 0.0 copy-start.1
  6.9 8.6 %own_frames.1 = (bf16[512,32,128]{2,1,0:T(8,128)(2,1)S(1)}, f32[8,128,512]{2,1,0:T(8,128)S(1)}) custom-call(s32[128,16384]{1,0:T(8,128)} %samples_ref.3, f32[8,512]{1,0:T(8,128)} %coef_ref.1, bf16[512,512]{1,0:T(8,128)(2,1)} %constant.16.clone.table_hbm.table_ref), custom_call_target="tpu_custom_call" | custom-call | tf_op jit(solution)/shard_map/own_frames/pallas_call | solution.py:288
  15.5 0.0 collective-permute-done.1.ahead_ref
  15.6 0.0 collective-permute-done.behind_ref
  15.6 0.0 copy-done
  15.6 0.0 copy-done.1
  15.6 1.1 %edge_frames.1 = bf16[512,32,128]{2,1,0:T(8,128)(2,1)S(1)} custom-call(f32[1]{0:T(128)} %bitcast.has_behind_ref, f32[1]{0:T(128)} %bitcast.1.has_own_ref, bf16[128,2048]{1,0:T(8,128)(2,1)S(1)} %collective-permute-done.behind_ref, bf16[128,1536]{1,0:T(8,128)(2,1)S(1)} %collective-permute-done.1.ahead_ref, ...), custom_call_target="tpu_custom_call", output_to_operand_aliasing={{}: (7, {})} | custom-call | tf_op jit(solution)/shard_map/edge_frames/pallas_call | solution.py:304
  16.7 60.6 %all_to_all.5 = bf16[128,4,32,128]{3,2,1,0:T(8,128)(2,1)S(1)} all-to-all(bf16[128,4,32,128]{3,2,1,0:T(8,128)(2,1)S(1)} %bitcast.5), channel_id=1, replica_groups=mesh['tm'=16,'input'=8] {'tm','input'}, dimensions={0} | all-to-all | bytes 8388608 | tf_op jit(solution)/shard_map/all_to_all | solution.py:321
  77.3 7.2 %correlate.1 = bf16[2,2,1024,1024]{3,2,1,0:T(8,128)(2,1)} custom-call(bf16[16,8,2,2,32,128]{5,4,3,2,1,0:T(8,128)(2,1)S(1)} %bitcast.4), custom_call_target="tpu_custom_call" | custom-call | tf_op jit(solution)/shard_map/correlate/pallas_call | solution.py:326
Async XLA Ops:
  1.5 14.0 %collective-permute-start = (bf16[128,2048]{1,0:T(8,128)(2,1)S(1)}, bf16[128,2048]{1,0:T(8,128)(2,1)S(1)}, u32[]{:S(2)}, u32[]{:S(2)}) collective-permute-start(bf16[128,2048]{1,0:T(8,128)(2,1)S(1)} %get-tuple-element.9), channel_id=1, source_target_pairs={{0,8},{8,16},{16,24},{24,32},{32,40},{40,48},{48,56},{56,64},{64,7... | collective-permute-start | bytes 1572872 | tf_op jit(solution)/shard_map/ppermute | solution.py:285
  1.6 14.0 %collective-permute-start.1 = (bf16[128,1536]{1,0:T(8,128)(2,1)S(1)}, bf16[128,1536]{1,0:T(8,128)(2,1)S(1)}, u32[]{:S(2)}, u32[]{:S(2)}) collective-permute-start(bf16[128,1536]{1,0:T(8,128)(2,1)S(1)} %get-tuple-element.10), channel_id=1, source_target_pairs={{8,0},{16,8},{24,16},{32,24},{40,32},{48,40},{56,48},{64,56},{72,6... | collective-permute-start | bytes 1179656 | tf_op jit(solution)/shard_map/ppermute | solution.py:286
  6.9 8.6 %copy-start = (bf16[512,512]{1,0:T(8,128)(2,1)S(1)}, bf16[512,512]{1,0:T(8,128)(2,1)}, u32[]{:S(2)}) copy-start(bf16[512,512]{1,0:T(8,128)(2,1)} %constant.16.clone.table_hbm.table_ref) | copy-start | bytes 1572868
  6.9 8.6 %copy-start.1 = (f32[8,512]{1,0:T(8,128)S(1)}, f32[8,512]{1,0:T(8,128)}, u32[]{:S(2)}) copy-start(f32[8,512]{1,0:T(8,128)} %coef_ref.1) | copy-start | bytes 49156

commit v8 on v7

--- a/solution.py
+++ b/solution.py
@@ -13,7 +13,7 @@
 BLOCK = 256
 ROWS = 16
 LANES = 128
-AHEAD = 3
+AHEAD = 2
 
 
 def dft_table(length):

time: 84.7 us -> 84.7 us (level)
  no operation moved by 1% of the time
where the time goes in v8:
time: 84.7 us; the launch traced here: 84.6 us
  blocking collectives  60.6 us (72%)
  Pallas kernels  18.4 us (22%)
  starting transfers between devices  5.42 us (6%)
    all_to_all x1, blocking collectives, local(): received = lax.all_to_all(outgoing, ('tm', 'input'), 0, 0, tiled=True)  60.6 us
    pallas_call x1, Pallas kernels, local(): pl.pallas_call(own_kernel, in_specs=[hbm, hbm, hbm], out_specs=[vmem, vme...  8.5 us
    pallas_call x1, Pallas kernels, local(): pl.pallas_call(correlate_kernel, in_specs=[vmem], out_specs=hbm, out_shap...  7.15 us
    ppermute x1, starting transfers between devices, local(): from_ahead = lax.ppermute(first, 'tm', [(b, a) for a, b in ring])  5.35 us
  transfers between devices with their start and end apart: 2, of which 0 were waited for; matrix products, arithmetic and copies ran while one was open for 0% of the time, Pallas kernels for 10%

profile of v8, /device:TPU:0, one launch (start us, length us, event | category | flops | bytes accessed | tf_op | source)
XLA Modules:
  0.0 84.6 jit_solution(6728704235853544594)
XLA Ops:
  0.0 1.5 %tails.1 = (bf16[128,2560]{1,0:T(8,128)(2,1)S(1)}, bf16[128,1024]{1,0:T(8,128)(2,1)S(1)}) custom-call(s32[128,16384]{1,0:T(8,128)} %samples_ref.3), custom_call_target="tpu_custom_call" | custom-call | tf_op jit(solution)/shard_map/tails/pallas_call | solution.py:269
  1.5 0.1 collective-permute-start
  1.6 5.3 %collective-permute-start.1 = (bf16[128,1024]{1,0:T(8,128)(2,1)S(1)}, bf16[128,1024]{1,0:T(8,128)(2,1)S(1)}, u32[]{:S(2)}, u32[]{:S(2)}) collective-permute-start(bf16[128,1024]{1,0:T(8,128)(2,1)S(1)} %get-tuple-element.10), channel_id=1, source_target_pairs={{8,0},{16,8},{24,16},{32,24},{40,32},{48,40},{56,48},{64,56},{72,6... | collective-permute-start | bytes 786440 | tf_op jit(solution)/shard_map/ppermute | solution.py:286
  6.9 0.0 copy-start
  6.9 0.0 copy-start.1
  6.9 8.5 %own_frames.1 = (bf16[512,32,128]{2,1,0:T(8,128)(2,1)S(1)}, f32[8,128,512]{2,1,0:T(8,128)S(1)}) custom-call(s32[128,16384]{1,0:T(8,128)} %samples_ref.3, f32[8,512]{1,0:T(8,128)} %coef_ref.1, bf16[512,512]{1,0:T(8,128)(2,1)} %constant.16.clone.table_hbm.table_ref), custom_call_target="tpu_custom_call" | custom-call | tf_op jit(solution)/shard_map/own_frames/pallas_call | solution.py:288
  15.4 0.0 collective-permute-done.1.ahead_ref
  15.4 0.0 collective-permute-done.behind_ref
  15.5 0.0 copy-done
  15.5 0.0 copy-done.1
  15.5 1.2 %edge_frames.1 = bf16[512,32,128]{2,1,0:T(8,128)(2,1)S(1)} custom-call(f32[1]{0:T(128)} %bitcast.has_behind_ref, f32[1]{0:T(128)} %bitcast.1.has_own_ref, bf16[128,2560]{1,0:T(8,128)(2,1)S(1)} %collective-permute-done.behind_ref, bf16[128,1024]{1,0:T(8,128)(2,1)S(1)} %collective-permute-done.1.ahead_ref, ...), custom_call_target="tpu_custom_call", output_to_operand_aliasing={{}: (7, {})} | custom-call | tf_op jit(solution)/shard_map/edge_frames/pallas_call | solution.py:304
  16.7 60.6 %all_to_all.5 = bf16[128,4,32,128]{3,2,1,0:T(8,128)(2,1)S(1)} all-to-all(bf16[128,4,32,128]{3,2,1,0:T(8,128)(2,1)S(1)} %bitcast.5), channel_id=1, replica_groups=mesh['tm'=16,'input'=8] {'tm','input'}, dimensions={0} | all-to-all | bytes 8388608 | tf_op jit(solution)/shard_map/all_to_all | solution.py:321
  77.3 7.1 %correlate.1 = bf16[2,2,1024,1024]{3,2,1,0:T(8,128)(2,1)} custom-call(bf16[16,8,2,2,32,128]{5,4,3,2,1,0:T(8,128)(2,1)S(1)} %bitcast.4), custom_call_target="tpu_custom_call" | custom-call | tf_op jit(solution)/shard_map/correlate/pallas_call | solution.py:326
Async XLA Ops:
  1.5 14.0 %collective-permute-start = (bf16[128,2560]{1,0:T(8,128)(2,1)S(1)}, bf16[128,2560]{1,0:T(8,128)(2,1)S(1)}, u32[]{:S(2)}, u32[]{:S(2)}) collective-permute-start(bf16[128,2560]{1,0:T(8,128)(2,1)S(1)} %get-tuple-element.9), channel_id=1, source_target_pairs={{0,8},{8,16},{16,24},{24,32},{32,40},{40,48},{48,56},{56,64},{64,7... | collective-permute-start | bytes 1966088 | tf_op jit(solution)/shard_map/ppermute | solution.py:285
  1.6 13.9 %collective-permute-start.1 = (bf16[128,1024]{1,0:T(8,128)(2,1)S(1)}, bf16[128,1024]{1,0:T(8,128)(2,1)S(1)}, u32[]{:S(2)}, u32[]{:S(2)}) collective-permute-start(bf16[128,1024]{1,0:T(8,128)(2,1)S(1)} %get-tuple-element.10), channel_id=1, source_target_pairs={{8,0},{16,8},{24,16},{32,24},{40,32},{48,40},{56,48},{64,56},{72,6... | collective-permute-start | bytes 786440 | tf_op jit(solution)/shard_map/ppermute | solution.py:286
  6.9 8.5 %copy-start = (bf16[512,512]{1,0:T(8,128)(2,1)S(1)}, bf16[512,512]{1,0:T(8,128)(2,1)}, u32[]{:S(2)}) copy-start(bf16[512,512]{1,0:T(8,128)(2,1)} %constant.16.clone.table_hbm.table_ref) | copy-start | bytes 1572868
  6.9 8.5 %copy-start.1 = (f32[8,512]{1,0:T(8,128)S(1)}, f32[8,512]{1,0:T(8,128)}, u32[]{:S(2)}) copy-start(f32[8,512]{1,0:T(8,128)} %coef_ref.1) | copy-start | bytes 49156

commit v9 on v8

--- a/solution.py
+++ b/solution.py
@@ -30,18 +30,20 @@
 
 
 def tails_kernel(samples_ref, last_ref, first_ref, last, first, sems):
-    count = samples_ref.shape[1]
-    copies = [
-        pltpu.make_async_copy(
-            samples_ref.at[:, pl.ds(count - last.shape[1], last.shape[1])], last, sems.at[0]
-        ),
-        pltpu.make_async_copy(samples_ref.at[:, pl.ds(0, first.shape[1])], first, sems.at[1]),
-    ]
-    for copy in copies:
-        copy.start()
-    for copy, source, target in zip(copies, (last, first), (last_ref, first_ref), strict=True):
+    inputs, count = samples_ref.shape
+    parts = sems.shape[0] // 2
+    step = inputs // parts
+    copies = []
+    for part in range(parts):
+        rows = pl.ds(part * step, step)
+        for held, target, start in ((last, last_ref, count - last.shape[1]), (first, first_ref, 0)):
+            source = samples_ref.at[rows, pl.ds(start, held.shape[1])]
+            copy = pltpu.make_async_copy(source, held.at[rows], sems.at[len(copies)])
+            copy.start()
+            copies.append((copy, slice(part * step, (part + 1) * step), held, target))
+    for copy, rows, held, target in copies:
         copy.wait()
-        target[...] = source[...].astype(jnp.float32).astype(jnp.bfloat16)
+        target[rows] = held[rows].astype(jnp.float32).astype(jnp.bfloat16)
 
 
 def transform_pair(filt, f, table_ref, spread):
@@ -191,7 +193,7 @@
     pack(spread, spectra_ref, 0, 0, 1)
 
 
-def correlate_kernel(recv_ref, out_ref, held, turned, swapped, stage, sems):
+def correlate_kernel(recv_ref, out_ref, held, turned, summed, less, stage, sems):
     tm_count, input_count, items, _, frames, inputs = recv_ref.shape
     half = tm_count * frames
     width = input_count * inputs
@@ -200,12 +202,15 @@
 
     def give(c, part, i, j, value):
         rows, cols = pl.ds(i, BLOCK), pl.ds(j, BLOCK)
-        stage[c, part, rows, cols] = value.astype(jnp.bfloat16)
+        stage[c, part, rows, cols] = value
         copy = pltpu.make_async_copy(
             stage.at[c, part, rows, cols], out_ref.at[c, part, rows, cols], sems.at[len(copies)]
         )
         copy.start()
         copies.append(copy)
+
+    def product(left, right):
+        return scale * jnp.dot(left, right, preferred_element_type=jnp.float32)
 
     for c in range(items):
         for r in range(2):
@@ -215,30 +220,25 @@
                     cols = slice(b * inputs, (b + 1) * inputs)
                     held[c, rows, cols] = recv_ref[a, b, c, r]
         turned[c] = held[c].T
-        swapped[c, :half] = -held[c, half:]
-        swapped[c, half:] = held[c, :half]
+        summed[c] = turned[c, :, :half] + turned[c, :, half:]
+        less[c] = held[c, :half] - held[c, half:]
         for i in range(0, width, BLOCK):
-            for j in range(i, width, BLOCK):
-                left = turned[c, i : i + BLOCK]
-                real = scale * jnp.dot(
-                    left, held[c, :, j : j + BLOCK], preferred_element_type=jnp.float32
-                )
-                if j > i:
-                    imag = scale * jnp.dot(
-                        left, swapped[c, :, j : j + BLOCK], preferred_element_type=jnp.float32
-                    )
-                else:
-                    cross = scale * jnp.dot(
-                        turned[c, i : i + BLOCK, half:],
-                        held[c, :half, j : j + BLOCK],
-                        preferred_element_type=jnp.float32,
-                    )
-                    imag = cross - cross.T
+            rows = slice(i, i + BLOCK)
+            real = product(turned[c, rows], held[c, :, rows])
+            cross = product(turned[c, rows, half:], held[c, :half, rows])
+            give(c, 0, i, i, real.astype(jnp.bfloat16))
+            give(c, 1, i, i, (cross - cross.T).astype(jnp.bfloat16))
+            for j in range(i + BLOCK, width, BLOCK):
+                cols = slice(j, j + BLOCK)
+                first = product(turned[c, rows, :half], held[c, :half, cols])
+                second = product(turned[c, rows, half:], held[c, half:, cols])
+                mixed = product(summed[c, rows], less[c, :, cols])
+                real = (first + second).astype(jnp.bfloat16)
+                imag = (mixed - first + second).astype(jnp.bfloat16)
                 give(c, 0, i, j, real)
                 give(c, 1, i, j, imag)
-                if j > i:
-                    give(c, 0, j, i, real.T)
-                    give(c, 1, j, i, -imag.T)
+                give(c, 0, j, i, real.T)
+                give(c, 1, j, i, (-imag).T)
     for copy in copies:
         copy.wait()
 
@@ -277,7 +277,7 @@
         scratch_shapes=[
             pltpu.VMEM((inputs, past), jnp.int32),
             pltpu.VMEM((inputs, ahead), jnp.int32),
-            pltpu.SemaphoreType.DMA((2,)),
+            pltpu.SemaphoreType.DMA((8,)),
         ],
         compiler_params=pltpu.CompilerParams(vmem_limit_bytes=8 << 20),
         name="tails",
@@ -331,7 +331,8 @@
         scratch_shapes=[
             pltpu.VMEM((items, depth, width), jnp.bfloat16),
             pltpu.VMEM((items, width, depth), jnp.bfloat16),
-            pltpu.VMEM((items, depth, width), jnp.bfloat16),
+            pltpu.VMEM((items, width, depth // 2), jnp.bfloat16),
+            pltpu.VMEM((items, depth // 2, width), jnp.bfloat16),
             pltpu.VMEM((items, 2, width, width), jnp.bfloat16),
             pltpu.SemaphoreType.DMA((2 * items * blocks,)),
         ],

time: 84.7 us -> 84.4 us (level)
  no operation moved by 1% of the time
where the time goes in v9:
time: 84.4 us; the launch traced here: 84.3 us
  blocking collectives  60.6 us (72%)
  Pallas kernels  18.1 us (21%)
  starting transfers between devices  5.42 us (6%)
    all_to_all x1, blocking collectives, local(): received = lax.all_to_all(outgoing, ('tm', 'input'), 0, 0, tiled=True)  60.6 us
    pallas_call x1, Pallas kernels, local(): pl.pallas_call(own_kernel, in_specs=[hbm, hbm, hbm], out_specs=[vmem, vme...  8.51 us
    pallas_call x1, Pallas kernels, local(): pl.pallas_call(correlate_kernel, in_specs=[vmem], out_specs=hbm, out_shap...  6.8 us
    ppermute x1, starting transfers between devices, local(): from_ahead = lax.ppermute(first, 'tm', [(b, a) for a, b in ring])  5.35 us
  transfers between devices with their start and end apart: 2, of which 0 were waited for; matrix products, arithmetic and copies ran while one was open for 0% of the time, Pallas kernels for 10%

profile of v9, /device:TPU:0, one launch (start us, length us, event | category | flops | bytes accessed | tf_op | source)
XLA Modules:
  0.0 84.3 jit_solution(12900776201861701117)
XLA Ops:
  0.0 1.5 %tails.1 = (bf16[128,2560]{1,0:T(8,128)(2,1)S(1)}, bf16[128,1024]{1,0:T(8,128)(2,1)S(1)}) custom-call(s32[128,16384]{1,0:T(8,128)} %samples_ref.3), custom_call_target="tpu_custom_call" | custom-call | tf_op jit(solution)/shard_map/tails/pallas_call | solution.py:269
  1.5 0.1 collective-permute-start
  1.6 5.3 %collective-permute-start.1 = (bf16[128,1024]{1,0:T(8,128)(2,1)S(1)}, bf16[128,1024]{1,0:T(8,128)(2,1)S(1)}, u32[]{:S(2)}, u32[]{:S(2)}) collective-permute-start(bf16[128,1024]{1,0:T(8,128)(2,1)S(1)} %get-tuple-element.10), channel_id=1, source_target_pairs={{8,0},{16,8},{24,16},{32,24},{40,32},{48,40},{56,48},{64,56},{72,6... | collective-permute-start | bytes 786440 | tf_op jit(solution)/shard_map/ppermute | solution.py:286
  7.0 0.0 copy-start
  7.0 0.0 copy-start.1
  7.0 8.5 %own_frames.1 = (bf16[512,32,128]{2,1,0:T(8,128)(2,1)S(1)}, f32[8,128,512]{2,1,0:T(8,128)S(1)}) custom-call(s32[128,16384]{1,0:T(8,128)} %samples_ref.3, f32[8,512]{1,0:T(8,128)} %coef_ref.1, bf16[512,512]{1,0:T(8,128)(2,1)} %constant.16.clone.table_hbm.table_ref), custom_call_target="tpu_custom_call" | custom-call | tf_op jit(solution)/shard_map/own_frames/pallas_call | solution.py:288
  15.5 0.0 collective-permute-done.1.ahead_ref
  15.5 0.0 collective-permute-done.behind_ref
  15.5 0.0 copy-done
  15.5 0.0 copy-done.1
  15.5 1.2 %edge_frames.1 = bf16[512,32,128]{2,1,0:T(8,128)(2,1)S(1)} custom-call(f32[1]{0:T(128)} %bitcast.has_behind_ref, f32[1]{0:T(128)} %bitcast.1.has_own_ref, bf16[128,2560]{1,0:T(8,128)(2,1)S(1)} %collective-permute-done.behind_ref, bf16[128,1024]{1,0:T(8,128)(2,1)S(1)} %collective-permute-done.1.ahead_ref, ...), custom_call_target="tpu_custom_call", output_to_operand_aliasing={{}: (7, {})} | custom-call | tf_op jit(solution)/shard_map/edge_frames/pallas_call | solution.py:304
  16.8 60.6 %all_to_all.5 = bf16[128,4,32,128]{3,2,1,0:T(8,128)(2,1)S(1)} all-to-all(bf16[128,4,32,128]{3,2,1,0:T(8,128)(2,1)S(1)} %bitcast.5), channel_id=1, replica_groups=mesh['tm'=16,'input'=8] {'tm','input'}, dimensions={0} | all-to-all | bytes 8388608 | tf_op jit(solution)/shard_map/all_to_all | solution.py:321
  77.3 6.8 %correlate.1 = bf16[2,2,1024,1024]{3,2,1,0:T(8,128)(2,1)} custom-call(bf16[16,8,2,2,32,128]{5,4,3,2,1,0:T(8,128)(2,1)S(1)} %bitcast.4), custom_call_target="tpu_custom_call" | custom-call | tf_op jit(solution)/shard_map/correlate/pallas_call | solution.py:326
Async XLA Ops:
  1.5 14.0 %collective-permute-start = (bf16[128,2560]{1,0:T(8,128)(2,1)S(1)}, bf16[128,2560]{1,0:T(8,128)(2,1)S(1)}, u32[]{:S(2)}, u32[]{:S(2)}) collective-permute-start(bf16[128,2560]{1,0:T(8,128)(2,1)S(1)} %get-tuple-element.9), channel_id=1, source_target_pairs={{0,8},{8,16},{16,24},{24,32},{32,40},{40,48},{48,56},{56,64},{64,7... | collective-permute-start | bytes 1966088 | tf_op jit(solution)/shard_map/ppermute | solution.py:285
  1.6 13.9 %collective-permute-start.1 = (bf16[128,1024]{1,0:T(8,128)(2,1)S(1)}, bf16[128,1024]{1,0:T(8,128)(2,1)S(1)}, u32[]{:S(2)}, u32[]{:S(2)}) collective-permute-start(bf16[128,1024]{1,0:T(8,128)(2,1)S(1)} %get-tuple-element.10), channel_id=1, source_target_pairs={{8,0},{16,8},{24,16},{32,24},{40,32},{48,40},{56,48},{64,56},{72,6... | collective-permute-start | bytes 786440 | tf_op jit(solution)/shard_map/ppermute | solution.py:286
  7.0 8.5 %copy-start = (bf16[512,512]{1,0:T(8,128)(2,1)S(1)}, bf16[512,512]{1,0:T(8,128)(2,1)}, u32[]{:S(2)}) copy-start(bf16[512,512]{1,0:T(8,128)(2,1)} %constant.16.clone.table_hbm.table_ref) | copy-start | bytes 1572868
  7.0 8.6 %copy-start.1 = (f32[8,512]{1,0:T(8,128)S(1)}, f32[8,512]{1,0:T(8,128)}, u32[]{:S(2)}) copy-start(f32[8,512]{1,0:T(8,128)} %coef_ref.1) | copy-start | bytes 49156

commit v10 on v8

--- a/solution.py
+++ b/solution.py
@@ -146,9 +146,10 @@
     for pair in range(pairs):
         transform_pair(filts[last % 2], 2 * pair, table_ref, spreads[last % 2])
         pack(spreads[(last - 1) % 2], spectra_ref, last - 1, pair, pairs)
-        filter_rows(0, pair * 2 * ROWS)
-        filter_rows(0, pair * 2 * ROWS + ROWS)
-    pack(spreads[last % 2], spectra_ref, last, 0, 1)
+        filter_rows(0, pair * ROWS)
+    for pair in range(pairs):
+        pack(spreads[last % 2], spectra_ref, last, pair, pairs)
+        filter_rows(0, (pairs + pair) * ROWS)
 
 
 def edge_kernel(
@@ -200,7 +201,7 @@
 
     def give(c, part, i, j, value):
         rows, cols = pl.ds(i, BLOCK), pl.ds(j, BLOCK)
-        stage[c, part, rows, cols] = value.astype(jnp.bfloat16)
+        stage[c, part, rows, cols] = value
         copy = pltpu.make_async_copy(
             stage.at[c, part, rows, cols], out_ref.at[c, part, rows, cols], sems.at[len(copies)]
         )
@@ -234,11 +235,13 @@
                         preferred_element_type=jnp.float32,
                     )
                     imag = cross - cross.T
+                real = real.astype(jnp.bfloat16)
+                imag = imag.astype(jnp.bfloat16)
                 give(c, 0, i, j, real)
                 give(c, 1, i, j, imag)
                 if j > i:
                     give(c, 0, j, i, real.T)
-                    give(c, 1, j, i, -imag.T)
+                    give(c, 1, j, i, (-imag).T)
     for copy in copies:
         copy.wait()
 

time: 84.7 us -> 84.8 us (level)
  no operation moved by 1% of the time
where the time goes in v10:
time: 84.8 us; the launch traced here: 84.6 us
  blocking collectives  60.6 us (71%)
  Pallas kernels  18.4 us (22%)
  starting transfers between devices  5.42 us (6%)
    all_to_all x1, blocking collectives, local(): received = lax.all_to_all(outgoing, ('tm', 'input'), 0, 0, tiled=True)  60.6 us
    pallas_call x1, Pallas kernels, local(): pl.pallas_call(own_kernel, in_specs=[hbm, hbm, hbm], out_specs=[vmem, vme...  8.5 us
    pallas_call x1, Pallas kernels, local(): pl.pallas_call(correlate_kernel, in_specs=[vmem], out_specs=hbm, out_shap...  7.16 us
    ppermute x1, starting transfers between devices, local(): from_ahead = lax.ppermute(first, 'tm', [(b, a) for a, b in ring])  5.35 us
  transfers between devices with their start and end apart: 2, of which 0 were waited for; matrix products, arithmetic and copies ran while one was open for 0% of the time, Pallas kernels for 10%

profile of v10, /device:TPU:0, one launch (start us, length us, event | category | flops | bytes accessed | tf_op | source)
XLA Modules:
  0.0 84.6 jit_solution(14432538572621051207)
XLA Ops:
  0.0 1.5 %tails.1 = (bf16[128,2560]{1,0:T(8,128)(2,1)S(1)}, bf16[128,1024]{1,0:T(8,128)(2,1)S(1)}) custom-call(s32[128,16384]{1,0:T(8,128)} %samples_ref.3), custom_call_target="tpu_custom_call" | custom-call | tf_op jit(solution)/shard_map/tails/pallas_call | solution.py:272
  1.5 0.1 collective-permute-start
  1.6 5.3 %collective-permute-start.1 = (bf16[128,1024]{1,0:T(8,128)(2,1)S(1)}, bf16[128,1024]{1,0:T(8,128)(2,1)S(1)}, u32[]{:S(2)}, u32[]{:S(2)}) collective-permute-start(bf16[128,1024]{1,0:T(8,128)(2,1)S(1)} %get-tuple-element.10), channel_id=1, source_target_pairs={{8,0},{16,8},{24,16},{32,24},{40,32},{48,40},{56,48},{64,56},{72,6... | collective-permute-start | bytes 786440 | tf_op jit(solution)/shard_map/ppermute | solution.py:289
  6.9 0.0 copy-start
  6.9 0.0 copy-start.1
  6.9 8.5 %own_frames.1 = (bf16[512,32,128]{2,1,0:T(8,128)(2,1)S(1)}, f32[8,128,512]{2,1,0:T(8,128)S(1)}) custom-call(s32[128,16384]{1,0:T(8,128)} %samples_ref.3, f32[8,512]{1,0:T(8,128)} %coef_ref.1, bf16[512,512]{1,0:T(8,128)(2,1)} %constant.16.clone.table_hbm.table_ref), custom_call_target="tpu_custom_call" | custom-call | tf_op jit(solution)/shard_map/own_frames/pallas_call | solution.py:291
  15.4 0.0 collective-permute-done.1.ahead_ref
  15.4 0.0 collective-permute-done.behind_ref
  15.5 0.0 copy-done
  15.5 0.0 copy-done.1
  15.5 1.2 %edge_frames.1 = bf16[512,32,128]{2,1,0:T(8,128)(2,1)S(1)} custom-call(f32[1]{0:T(128)} %bitcast.has_behind_ref, f32[1]{0:T(128)} %bitcast.1.has_own_ref, bf16[128,2560]{1,0:T(8,128)(2,1)S(1)} %collective-permute-done.behind_ref, bf16[128,1024]{1,0:T(8,128)(2,1)S(1)} %collective-permute-done.1.ahead_ref, ...), custom_call_target="tpu_custom_call", output_to_operand_aliasing={{}: (7, {})} | custom-call | tf_op jit(solution)/shard_map/edge_frames/pallas_call | solution.py:307
  16.7 60.6 %all_to_all.5 = bf16[128,4,32,128]{3,2,1,0:T(8,128)(2,1)S(1)} all-to-all(bf16[128,4,32,128]{3,2,1,0:T(8,128)(2,1)S(1)} %bitcast.5), channel_id=1, replica_groups=mesh['tm'=16,'input'=8] {'tm','input'}, dimensions={0} | all-to-all | bytes 8388608 | tf_op jit(solution)/shard_map/all_to_all | solution.py:324
  77.3 7.2 %correlate.1 = bf16[2,2,1024,1024]{3,2,1,0:T(8,128)(2,1)} custom-call(bf16[16,8,2,2,32,128]{5,4,3,2,1,0:T(8,128)(2,1)S(1)} %bitcast.4), custom_call_target="tpu_custom_call" | custom-call | tf_op jit(solution)/shard_map/correlate/pallas_call | solution.py:329
Async XLA Ops:
  1.5 14.0 %collective-permute-start = (bf16[128,2560]{1,0:T(8,128)(2,1)S(1)}, bf16[128,2560]{1,0:T(8,128)(2,1)S(1)}, u32[]{:S(2)}, u32[]{:S(2)}) collective-permute-start(bf16[128,2560]{1,0:T(8,128)(2,1)S(1)} %get-tuple-element.9), channel_id=1, source_target_pairs={{0,8},{8,16},{16,24},{24,32},{32,40},{40,48},{48,56},{56,64},{64,7... | collective-permute-start | bytes 1966088 | tf_op jit(solution)/shard_map/ppermute | solution.py:288
  1.6 13.9 %collective-permute-start.1 = (bf16[128,1024]{1,0:T(8,128)(2,1)S(1)}, bf16[128,1024]{1,0:T(8,128)(2,1)S(1)}, u32[]{:S(2)}, u32[]{:S(2)}) collective-permute-start(bf16[128,1024]{1,0:T(8,128)(2,1)S(1)} %get-tuple-element.10), channel_id=1, source_target_pairs={{8,0},{16,8},{24,16},{32,24},{40,32},{48,40},{56,48},{64,56},{72,6... | collective-permute-start | bytes 786440 | tf_op jit(solution)/shard_map/ppermute | solution.py:289
  6.9 8.5 %copy-start = (bf16[512,512]{1,0:T(8,128)(2,1)S(1)}, bf16[512,512]{1,0:T(8,128)(2,1)}, u32[]{:S(2)}) copy-start(bf16[512,512]{1,0:T(8,128)(2,1)} %constant.16.clone.table_hbm.table_ref) | copy-start | bytes 1572868
  6.9 8.5 %copy-start.1 = (f32[8,512]{1,0:T(8,128)S(1)}, f32[8,512]{1,0:T(8,128)}, u32[]{:S(2)}) copy-start(f32[8,512]{1,0:T(8,128)} %coef_ref.1) | copy-start | bytes 49156

commit v11 on v8

--- a/solution.py
+++ b/solution.py
@@ -200,7 +200,7 @@
 
     def give(c, part, i, j, value):
         rows, cols = pl.ds(i, BLOCK), pl.ds(j, BLOCK)
-        stage[c, part, rows, cols] = value.astype(jnp.bfloat16)
+        stage[c, part, rows, cols] = value
         copy = pltpu.make_async_copy(
             stage.at[c, part, rows, cols], out_ref.at[c, part, rows, cols], sems.at[len(copies)]
         )
@@ -234,11 +234,13 @@
                         preferred_element_type=jnp.float32,
                     )
                     imag = cross - cross.T
+                real = real.astype(jnp.bfloat16)
+                imag = imag.astype(jnp.bfloat16)
                 give(c, 0, i, j, real)
                 give(c, 1, i, j, imag)
                 if j > i:
                     give(c, 0, j, i, real.T)
-                    give(c, 1, j, i, -imag.T)
+                    give(c, 1, j, i, (-imag).T)
     for copy in copies:
         copy.wait()
 

time: 84.7 us -> 84.8 us (level)
  no operation moved by 1% of the time
where the time goes in v11:
time: 84.8 us; the launch traced here: 84.6 us
  blocking collectives  60.6 us (71%)
  Pallas kernels  18.4 us (22%)
  starting transfers between devices  5.42 us (6%)
    all_to_all x1, blocking collectives, local(): received = lax.all_to_all(outgoing, ('tm', 'input'), 0, 0, tiled=True)  60.6 us
    pallas_call x1, Pallas kernels, local(): pl.pallas_call(own_kernel, in_specs=[hbm, hbm, hbm], out_specs=[vmem, vme...  8.5 us
    pallas_call x1, Pallas kernels, local(): pl.pallas_call(correlate_kernel, in_specs=[vmem], out_specs=hbm, out_shap...  7.16 us
    ppermute x1, starting transfers between devices, local(): from_ahead = lax.ppermute(first, 'tm', [(b, a) for a, b in ring])  5.35 us
  transfers between devices with their start and end apart: 2, of which 0 were waited for; matrix products, arithmetic and copies ran while one was open for 0% of the time, Pallas kernels for 10%

profile of v11, /device:TPU:0, one launch (start us, length us, event | category | flops | bytes accessed | tf_op | source)
XLA Modules:
  0.0 84.6 jit_solution(14432538572621051207)
XLA Ops:
  0.0 1.5 %tails.1 = (bf16[128,2560]{1,0:T(8,128)(2,1)S(1)}, bf16[128,1024]{1,0:T(8,128)(2,1)S(1)}) custom-call(s32[128,16384]{1,0:T(8,128)} %samples_ref.3), custom_call_target="tpu_custom_call" | custom-call | tf_op jit(solution)/shard_map/tails/pallas_call | solution.py:271
  1.5 0.1 collective-permute-start
  1.6 5.3 %collective-permute-start.1 = (bf16[128,1024]{1,0:T(8,128)(2,1)S(1)}, bf16[128,1024]{1,0:T(8,128)(2,1)S(1)}, u32[]{:S(2)}, u32[]{:S(2)}) collective-permute-start(bf16[128,1024]{1,0:T(8,128)(2,1)S(1)} %get-tuple-element.10), channel_id=1, source_target_pairs={{8,0},{16,8},{24,16},{32,24},{40,32},{48,40},{56,48},{64,56},{72,6... | collective-permute-start | bytes 786440 | tf_op jit(solution)/shard_map/ppermute | solution.py:288
  6.9 0.0 copy-start
  6.9 0.0 copy-start.1
  6.9 8.5 %own_frames.1 = (bf16[512,32,128]{2,1,0:T(8,128)(2,1)S(1)}, f32[8,128,512]{2,1,0:T(8,128)S(1)}) custom-call(s32[128,16384]{1,0:T(8,128)} %samples_ref.3, f32[8,512]{1,0:T(8,128)} %coef_ref.1, bf16[512,512]{1,0:T(8,128)(2,1)} %constant.16.clone.table_hbm.table_ref), custom_call_target="tpu_custom_call" | custom-call | tf_op jit(solution)/shard_map/own_frames/pallas_call | solution.py:290
  15.4 0.0 collective-permute-done.1.ahead_ref
  15.4 0.0 collective-permute-done.behind_ref
  15.5 0.0 copy-done
  15.5 0.0 copy-done.1
  15.5 1.2 %edge_frames.1 = bf16[512,32,128]{2,1,0:T(8,128)(2,1)S(1)} custom-call(f32[1]{0:T(128)} %bitcast.has_behind_ref, f32[1]{0:T(128)} %bitcast.1.has_own_ref, bf16[128,2560]{1,0:T(8,128)(2,1)S(1)} %collective-permute-done.behind_ref, bf16[128,1024]{1,0:T(8,128)(2,1)S(1)} %collective-permute-done.1.ahead_ref, ...), custom_call_target="tpu_custom_call", output_to_operand_aliasing={{}: (7, {})} | custom-call | tf_op jit(solution)/shard_map/edge_frames/pallas_call | solution.py:306
  16.7 60.6 %all_to_all.5 = bf16[128,4,32,128]{3,2,1,0:T(8,128)(2,1)S(1)} all-to-all(bf16[128,4,32,128]{3,2,1,0:T(8,128)(2,1)S(1)} %bitcast.5), channel_id=1, replica_groups=mesh['tm'=16,'input'=8] {'tm','input'}, dimensions={0} | all-to-all | bytes 8388608 | tf_op jit(solution)/shard_map/all_to_all | solution.py:323
  77.3 7.2 %correlate.1 = bf16[2,2,1024,1024]{3,2,1,0:T(8,128)(2,1)} custom-call(bf16[16,8,2,2,32,128]{5,4,3,2,1,0:T(8,128)(2,1)S(1)} %bitcast.4), custom_call_target="tpu_custom_call" | custom-call | tf_op jit(solution)/shard_map/correlate/pallas_call | solution.py:328
Async XLA Ops:
  1.5 14.0 %collective-permute-start = (bf16[128,2560]{1,0:T(8,128)(2,1)S(1)}, bf16[128,2560]{1,0:T(8,128)(2,1)S(1)}, u32[]{:S(2)}, u32[]{:S(2)}) collective-permute-start(bf16[128,2560]{1,0:T(8,128)(2,1)S(1)} %get-tuple-element.9), channel_id=1, source_target_pairs={{0,8},{8,16},{16,24},{24,32},{32,40},{40,48},{48,56},{56,64},{64,7... | collective-permute-start | bytes 1966088 | tf_op jit(solution)/shard_map/ppermute | solution.py:287
  1.6 13.9 %collective-permute-start.1 = (bf16[128,1024]{1,0:T(8,128)(2,1)S(1)}, bf16[128,1024]{1,0:T(8,128)(2,1)S(1)}, u32[]{:S(2)}, u32[]{:S(2)}) collective-permute-start(bf16[128,1024]{1,0:T(8,128)(2,1)S(1)} %get-tuple-element.10), channel_id=1, source_target_pairs={{8,0},{16,8},{24,16},{32,24},{40,32},{48,40},{56,48},{64,56},{72,6... | collective-permute-start | bytes 786440 | tf_op jit(solution)/shard_map/ppermute | solution.py:288
  6.9 8.5 %copy-start = (bf16[512,512]{1,0:T(8,128)(2,1)S(1)}, bf16[512,512]{1,0:T(8,128)(2,1)}, u32[]{:S(2)}) copy-start(bf16[512,512]{1,0:T(8,128)(2,1)} %constant.16.clone.table_hbm.table_ref) | copy-start | bytes 1572868
  6.9 8.5 %copy-start.1 = (f32[8,512]{1,0:T(8,128)S(1)}, f32[8,512]{1,0:T(8,128)}, u32[]{:S(2)}) copy-start(f32[8,512]{1,0:T(8,128)} %coef_ref.1) | copy-start | bytes 49156
